TPU v7x, 32 devices: a whole 2x2x4 slice. The times are simulated.
32 devices in a mesh: shard: 4 (over z), ctx: 2 (over x), tp: 4 (over y, core).
Axes of the slice: x: 2, y: 2, z: 4, core: 2. Of those that a mesh axis runs over, the one named last changes fastest.
Arguments:
- tokens: bfloat16 [4, 1024, 768], P('shard', 'ctx'), may hold values from -6 to 6
- segment_ids: int32 [4, 1024], P('shard', 'ctx'), may hold values from 0 to 15, never falling along the last dimension, each value on 1 to 512 neighbouring positions
- valid_mask: int32 [4, 1024], P('shard', 'ctx'), may hold values from 0 to 1, as said below
- qkv_weight: bfloat16 [3, 768, 768], P(None, ('shard', 'ctx'), 'tp'), may hold values from -0.21875 to 0.21875
- qv_bias: float32 [2, 768], P(None, 'tp'), may hold values from -0.4375 to 0.4375
- out_weight: bfloat16 [768, 768], P('tp', ('shard', 'ctx')), may hold values from -2.5 to 2.5
- out_bias: float32 [768], replicated, may hold values from -1.5 to 1.5
- norm1_gain: float32 [768], replicated, may hold values from 0.5 to 1.5
- norm1_shift: float32 [768], replicated, may hold values from -1.5 to 1.5
- in_weight: bfloat16 [768, 3072], P(('shard', 'ctx'), 'tp'), may hold values from -0.21875 to 0.21875
- in_bias: float32 [3072], P('tp'), may hold values from -4 to 4
- down_weight: bfloat16 [3072, 768], P('tp', ('shard', 'ctx')), may hold values from -0.109375 to 0.109375
- down_bias: float32 [768], replicated, may hold values from -1.5 to 1.5
- norm2_gain: float32 [768], replicated, may hold values from 0.5 to 1.5
- norm2_shift: float32 [768], replicated, may hold values from -1.5 to 1.5
- out_cotangent: float32 [4, 1024, 768], P('shard', 'ctx'), may hold values from -6 to 6
Outputs:
- layer_out: bfloat16 [4, 1024, 768], P('shard', 'ctx')
- tokens_grad: float32 [4, 1024, 768], P('shard', 'ctx')
- qkv_weight_grad: float32 [3, 768, 768], P(None, ('shard', 'ctx'), 'tp')
- qv_bias_grad: float32 [2, 768], P(None, 'tp')
- out_weight_grad: float32 [768, 768], P('tp', ('shard', 'ctx'))
- out_bias_grad: float32 [768], replicated
- norm1_gain_grad: float32 [768], replicated
- norm1_shift_grad: float32 [768], replicated
- in_weight_grad: float32 [768, 3072], P(('shard', 'ctx'), 'tp')
- in_bias_grad: float32 [3072], P('tp')
- down_weight_grad: float32 [3072, 768], P('tp', ('shard', 'ctx'))
- down_bias_grad: float32 [768], replicated
- norm2_gain_grad: float32 [768], replicated
- norm2_shift_grad: float32 [768], replicated
- stream_rms: float32 [3], replicated
Inputs may be any that keep to these rules, and one draw needn't show every extreme that they name: `segment_ids`: in each sequence the document numbers never fall; each of the 16 documents holds 1 to 512 tokens, and one holds exactly 512. In each sequence the tokens with valid_mask 1 are a leading run of 512 to 1024 positions.
All inputs are finite; a program needn't handle non-finite values.
Results may differ from a plain program's by a relative error of at most 0.012.
Values may be sent and summed in bfloat16 or wider, within the bound.
A program may use at most 128 MiB of HBM per device.

v0:
```python
import jax
import jax.numpy as jnp
from jax import lax
from jax.sharding import PartitionSpec as P

HEAD_DIM = 64


norm_eps = 1e-12
masked_score = -1e30


def layer_norm(rows, gain, shift):
    mean = jnp.mean(rows, axis=-1, keepdims=True)
    centred = rows - mean
    spread = jnp.mean(centred * centred, axis=-1, keepdims=True)
    return centred * lax.rsqrt(spread + norm_eps) * gain + shift


def gelu_tanh(value):
    return jax.nn.gelu(value, approximate=True)


def allowed_pairs(query_seg, query_pos, key_seg, key_valid, key_pos):
    same = query_seg[:, None] == key_seg[None, :]
    usable = (key_valid[None, :] == 1) | (query_pos[:, None] == key_pos[None, :])
    return same & usable


def scaled_scores(left, right):
    return jnp.einsum("ae,be->ab", left, right, preferred_element_type=jnp.float32) * 0.125


def softmax_parts(scores, mask):
    masked = jnp.where(mask, scores, masked_score)
    top = jnp.max(masked, axis=1)
    weights = jnp.where(mask, jnp.exp(masked - top[:, None]), 0.0)
    return (top, jnp.sum(weights, axis=1), weights)


def rebuilt_probs(scores, mask, top, total):
    masked = jnp.where(mask, scores, masked_score)
    weights = jnp.where(mask, jnp.exp(masked - top[:, None]), 0.0)
    return weights / total[:, None]


def body(
    tokens,
    segment_ids,
    valid_mask,
    qkv_weight,
    qv_bias,
    out_weight,
    out_bias,
    norm1_gain,
    norm1_shift,
    in_weight,
    in_bias,
    down_weight,
    down_bias,
    norm2_gain,
    norm2_shift,
    out_cotangent,
):
    seqs_here, piece, width = tokens.shape
    rows = seqs_here * piece
    cols = qkv_weight.shape[2]
    heads_here = cols // HEAD_DIM
    w_qkv, w_out, w_in, w_down = (
        lax.all_gather(qkv_weight, ("shard", "ctx"), axis=1, tiled=True),
        lax.all_gather(out_weight, ("shard", "ctx"), axis=1, tiled=True),
        lax.all_gather(in_weight, ("shard", "ctx"), axis=0, tiled=True),
        lax.all_gather(down_weight, ("shard", "ctx"), axis=1, tiled=True),
    )
    flat = tokens.reshape(rows, width)
    projected = jnp.einsum("nd,jdc->jnc", flat, w_qkv, preferred_element_type=jnp.float32)
    queries = (projected[0] + qv_bias[0]).astype(jnp.bfloat16).reshape(seqs_here, piece, cols)
    keys = projected[1].astype(jnp.bfloat16).reshape(seqs_here, piece, cols)
    values = (projected[2] + qv_bias[1]).astype(jnp.bfloat16).reshape(seqs_here, piece, cols)
    marks = lax.all_gather(jnp.stack([segment_ids, valid_mask]), "ctx", axis=2, tiled=True)
    kv_all = lax.all_gather(jnp.stack([keys, values]), "ctx", axis=2, tiled=True)
    seq_len = kv_all.shape[2]
    own_pos = lax.axis_index("ctx") * piece + lax.iota(jnp.int32, piece)
    all_pos = lax.iota(jnp.int32, seq_len)
    seq = 0
    mask = allowed_pairs(segment_ids[seq], own_pos, marks[0, seq], marks[1, seq], all_pos)
    masks = [mask]
    head_tops = []
    head_totals = []
    head_out = []
    for head in range(heads_here):
        span = slice(head * HEAD_DIM, (head + 1) * HEAD_DIM)
        scores = scaled_scores(queries[seq, :, span], kv_all[0, seq, :, span])
        top, total, weights = softmax_parts(scores, mask)
        probs = (weights / total[:, None]).astype(jnp.bfloat16)
        head_out.append(jnp.dot(probs, kv_all[1, seq, :, span], preferred_element_type=jnp.float32))
        head_tops.append(top)
        head_totals.append(total)
    context_parts = [jnp.concatenate(head_out, axis=1)]
    seq_tops = [jnp.stack(head_tops)]
    seq_totals = [jnp.stack(head_totals)]
    context = jnp.stack(context_parts).reshape(rows, cols).astype(jnp.bfloat16)
    top_all = jnp.stack(seq_tops)
    total_all = jnp.stack(seq_totals)
    attn = lax.psum(jnp.dot(context, w_out, preferred_element_type=jnp.float32), "tp") + out_bias
    hidden, norm1_back = jax.vjp(
        layer_norm, flat.astype(jnp.float32) + attn, norm1_gain, norm1_shift
    )
    hidden_low = hidden.astype(jnp.bfloat16)
    pre = jnp.dot(hidden_low, w_in, preferred_element_type=jnp.float32) + in_bias
    act, gelu_back = jax.vjp(gelu_tanh, pre)
    act_low = act.astype(jnp.bfloat16)
    ffn = lax.psum(jnp.dot(act_low, w_down, preferred_element_type=jnp.float32), "tp") + down_bias
    out_rows, norm2_back = jax.vjp(layer_norm, hidden + ffn, norm2_gain, norm2_shift)
    layer_out = out_rows.astype(jnp.bfloat16).reshape(seqs_here, piece, width)
    w_qkv, w_out, w_in, w_down = (
        lax.all_gather(qkv_weight, ("shard", "ctx"), axis=1, tiled=True),
        lax.all_gather(out_weight, ("shard", "ctx"), axis=1, tiled=True),
        lax.all_gather(in_weight, ("shard", "ctx"), axis=0, tiled=True),
        lax.all_gather(down_weight, ("shard", "ctx"), axis=1, tiled=True),
    )
    d_resid2, d_gain2, d_shift2 = norm2_back(out_cotangent.reshape(rows, width))
    d_ffn = d_resid2.astype(jnp.bfloat16)
    d_down_bias = jnp.sum(d_ffn.astype(jnp.float32), axis=0)
    g_down = jnp.einsum("nf,nd->fd", act_low, d_ffn, preferred_element_type=jnp.float32)
    d_act = jnp.einsum("nd,fd->nf", d_ffn, w_down, preferred_element_type=jnp.float32)
    d_pre = gelu_back(d_act)[0].astype(jnp.bfloat16)
    d_in_bias = jnp.sum(d_pre.astype(jnp.float32), axis=0)
    g_in = jnp.einsum("nd,nf->df", hidden_low, d_pre, preferred_element_type=jnp.float32)
    d_hidden = d_resid2 + lax.psum(
        jnp.einsum("nf,df->nd", d_pre, w_in, preferred_element_type=jnp.float32), "tp"
    )
    d_resid1, d_gain1, d_shift1 = norm1_back(d_hidden)
    d_attn = d_resid1.astype(jnp.bfloat16)
    d_out_bias = jnp.sum(d_attn.astype(jnp.float32), axis=0)
    g_out = jnp.einsum("nc,nd->cd", context, d_attn, preferred_element_type=jnp.float32)
    d_context = (
        jnp.einsum("nd,cd->nc", d_attn, w_out, preferred_element_type=jnp.float32)
        .astype(jnp.bfloat16)
        .reshape(seqs_here, piece, cols)
    )
    delta_parts = []
    seq = 0
    dq_heads = []
    dk_heads = []
    dv_heads = []
    delta_heads = []
    for head in range(heads_here):
        span = slice(head * HEAD_DIM, (head + 1) * HEAD_DIM)
        q_head = queries[seq, :, span]
        k_every = kv_all[0, seq, :, span]
        d_head = d_context[seq, :, span]
        probs = rebuilt_probs(
            scaled_scores(q_head, k_every), masks[seq], top_all[seq, head], total_all[seq, head]
        )
        d_probs = jnp.einsum(
            "qe,ke->qk", d_head, kv_all[1, seq, :, span], preferred_element_type=jnp.float32
        )
        delta = jnp.sum(probs * d_probs, axis=1)
        d_scores = (probs * (d_probs - delta[:, None])).astype(jnp.bfloat16)
        dq_heads.append(jnp.dot(d_scores, k_every, preferred_element_type=jnp.float32) * 0.125)
        delta_heads.append(delta)
        dk_heads.append(
            jnp.einsum("qk,qe->ke", d_scores, q_head, preferred_element_type=jnp.float32) * 0.125
        )
        dv_heads.append(
            jnp.einsum(
                "qk,qe->ke", probs.astype(jnp.bfloat16), d_head, preferred_element_type=jnp.float32
            )
        )
    query_parts = [jnp.concatenate(dq_heads, axis=1)]
    delta_parts.append(jnp.stack(delta_heads))
    key_parts = [jnp.concatenate(dk_heads, axis=1)]
    value_parts = [jnp.concatenate(dv_heads, axis=1)]
    d_queries = jnp.stack(query_parts).reshape(rows, cols).astype(jnp.bfloat16)
    key_sums, value_sums = (
        lax.psum_scatter(jnp.stack(key_parts), "ctx", scatter_dimension=1, tiled=True),
        lax.psum_scatter(jnp.stack(value_parts), "ctx", scatter_dimension=1, tiled=True),
    )
    d_keys = key_sums.reshape(rows, cols).astype(jnp.bfloat16)
    d_values = value_sums.reshape(rows, cols).astype(jnp.bfloat16)
    d_proj = jnp.stack([d_queries, d_keys, d_values])
    g_qkv = jnp.einsum("nd,jnc->jdc", flat, d_proj, preferred_element_type=jnp.float32)
    d_qv_bias = jnp.stack(
        [
            jnp.sum(d_queries.astype(jnp.float32), axis=0),
            jnp.sum(d_values.astype(jnp.float32), axis=0),
        ]
    )
    d_flat = d_resid1 + lax.psum(
        jnp.einsum("jnc,jdc->nd", d_proj, w_qkv, preferred_element_type=jnp.float32), "tp"
    )
    tokens_grad = d_flat.reshape(seqs_here, piece, width)
    g_qkv_own, g_out_own, g_in_own, g_down_own = (
        lax.psum_scatter(g_qkv, ("shard", "ctx"), scatter_dimension=1, tiled=True),
        lax.psum_scatter(g_out, ("shard", "ctx"), scatter_dimension=1, tiled=True),
        lax.psum_scatter(g_in, ("shard", "ctx"), scatter_dimension=0, tiled=True),
        lax.psum_scatter(g_down, ("shard", "ctx"), scatter_dimension=1, tiled=True),
    )
    valid_rows = valid_mask.reshape(rows, 1).astype(jnp.float32)
    x_rows = flat.astype(jnp.float32)
    stats = jnp.stack(
        [
            jnp.sum(valid_rows * x_rows * x_rows),
            jnp.sum(valid_rows * attn * attn),
            jnp.sum(valid_rows * ffn * ffn),
            jnp.sum(valid_rows),
        ]
    )
    summed = lax.psum(
        (
            d_qv_bias,
            d_out_bias,
            d_gain1,
            d_shift1,
            d_in_bias,
            d_down_bias,
            d_gain2,
            d_shift2,
            stats,
        ),
        ("shard", "ctx"),
    )
    totals = summed[8]
    stream_rms = jnp.sqrt(totals[:3] / (totals[3] * width))
    return (
        layer_out,
        tokens_grad,
        g_qkv_own,
        summed[0],
        g_out_own,
        summed[1],
        summed[2],
        summed[3],
        g_in_own,
        summed[4],
        g_down_own,
        summed[5],
        summed[6],
        summed[7],
        stream_rms,
    )


def solution(mesh):
    return jax.shard_map(
        body,
        mesh=mesh,
        in_specs=(
            P("shard", "ctx", None),
            P("shard", "ctx"),
            P("shard", "ctx"),
            P(None, ("shard", "ctx"), "tp"),
            P(None, "tp"),
            P("tp", ("shard", "ctx")),
            P(),
            P(),
            P(),
            P(("shard", "ctx"), "tp"),
            P("tp"),
            P("tp", ("shard", "ctx")),
            P(),
            P(),
            P(),
            P("shard", "ctx", None),
        ),
        out_specs=(
            P("shard", "ctx", None),
            P("shard", "ctx", None),
            P(None, ("shard", "ctx"), "tp"),
            P(None, "tp"),
            P("tp", ("shard", "ctx")),
            P(),
            P(),
            P(),
            P(("shard", "ctx"), "tp"),
            P("tp"),
            P("tp", ("shard", "ctx")),
            P(),
            P(),
            P(),
            P(),
        ),
        check_vma=False,
    )
```

profile of v0, /device:TPU:0, one launch (start us, length us, event | category | flops | bytes accessed | tf_op | source)
XLA Modules:
  0.0 687.0 jit_solution(15073184442933198201)
XLA Ops:
  8.8 5.2 all_gather.22
  15.9 38.3 %all_gather.23 = bf16[3,768,192]{2,0,1:T(4,128)(2,1)S(1)} all-gather(bf16[3,96,192]{2,0,1:T(4,128)(2,1)S(1)} %copy.34), channel_id=1, replica_groups=mesh['shard'=4,'ctx'=2,'tp'=4] {'shard','ctx'}, dimensions={1}, use_global_device_ids=true | all-gather | bytes 995328 | tf_op jit(solution)/shard_map/all_gather | solution.py:70
  55.7 8.5 %all_gather.24 = bf16[2,1,1024,192]{2,3,1,0:T(8,128)(2,1)S(1)} all-gather(bf16[2,1,512,192]{2,3,1,0:T(8,128)(2,1)S(1)} %pad_maximum_fusion.1), channel_id=1, replica_groups=mesh['shard'=4,'ctx'=2,'tp'=4] {'ctx'}, dimensions={2}, use_global_device_ids=true | all-gather | bytes 1179648 | tf_op jit(solution)/shard_map/all_gather | solution.py:81
  64.2 2.2 fusion.65
  66.4 2.2 fusion.64
  68.6 2.2 fusion.63
  70.9 31.2 %all_gather.25 = bf16[192,768]{0,1:T(8,128)(2,1)S(1)} all-gather(bf16[192,96]{0,1:T(8,128)(2,1)S(1)} %copy.36), channel_id=1, replica_groups=mesh['shard'=4,'ctx'=2,'tp'=4] {'shard','ctx'}, dimensions={1}, use_global_device_ids=true | all-gather | bytes 331776 | tf_op jit(solution)/shard_map/all_gather | solution.py:71
  102.1 4.2 fusion.13
  110.7 1.6 fusion.39
  113.6 41.2 %all-reduce.6.cloned.1.call-done = f32[512,768]{1,0:T(8,128)} async-done(((f32[512,768]{1,0:T(8,128)}), f32[512,768]{1,0:T(8,128)}) %all-reduce.6.cloned.1.call-update) | async-done | bytes 1572880 | tf_op jit(solution)/shard_map/psum | solution.py:105
  154.8 1.7 fusion.59
  157.2 3.3 convolution_add_fusion
  160.5 37.3 %all-gather.5.cloned.1.call-done = bf16[768,768]{0,1:T(8,128)(2,1)} async-done(((bf16[768,96]{0,1:T(8,128)(2,1)}), bf16[768,768]{0,1:T(8,128)(2,1)}) %all-gather.5.cloned.1.call-update) | async-done | bytes 1179664 | tf_op jit(solution)/shard_map/all_gather | solution.py:73
  197.8 4.0 fusion.48
  202.1 1.4 convert_element_type.154
  203.5 39.9 %all-reduce.8.cloned.1.call-done = f32[512,768]{1,0:T(8,128)} async-done(((f32[512,768]{1,0:T(8,128)}), f32[512,768]{1,0:T(8,128)}) %all-reduce.8.cloned.1.call-update) | async-done | bytes 1572880 | tf_op jit(solution)/shard_map/psum | solution.py:113
  243.3 3.6 fusion.9
  249.5 1.6 fusion.57
  251.9 1.3 copy-done.75
  253.2 2.2 convert_reduce_fusion.1
  256.3 2.0 fusion.66
  260.9 40.4 %all-reduce.10.cloned.1.call-done = f32[512,768]{1,0:T(8,128)} async-done(((f32[512,768]{1,0:T(8,128)}), f32[512,768]{1,0:T(8,128)}) %all-reduce.10.cloned.1.call-update) | async-done | bytes 1572880 | tf_op jit(solution)/shard_map/psum | solution.py:130
  301.3 3.3 multiply_reduce_fusion.3
  309.6 2.8 multiply_reduce_fusion.2
  317.9 2.0 fusion.25
  320.4 1.3 copy-done.9
  323.1 2.6 convolution_bitcast_fusion.3
  325.8 1.8 fusion.20
  327.6 1.7 fusion.19
  329.3 1.3 fusion.18
  330.6 4.6 reduce-scatter.11.cloned.1.call-done
  336.3 18.6 %reduce-scatter.13.cloned.1.call-done = f32[1,512,192]{1,2,0:T(8,128)} async-done(((f32[1,1024,192]{1,2,0:T(8,128)}), f32[1,512,192]{1,2,0:T(8,128)}) %reduce-scatter.13.cloned.1.call-update) | async-done | bytes 393232 | tf_op jit(solution)/shard_map/reduce_scatter | solution.py:178
  354.9 1.7 convert_reduce_fusion.3
  357.3 3.4 convolution_bitcast_fusion.1
  360.8 3.1 convolution_bitcast_fusion
  363.9 4.2 copy.39
  368.1 4.7 reshape.271
  373.5 3.5 fusion.49
  378.1 3.8 fusion.47
  383.3 2.6 pad_maximum_fusion.6
  386.0 34.5 %reduce-scatter.21.cloned.1.call-done = f32[96,192]{1,0:T(8,128)} async-done(((f32[768,192]{1,0:T(8,128)}), f32[96,192]{1,0:T(8,128)}) %reduce-scatter.21.cloned.1.call-update) | async-done | bytes 73744
  420.5 1.6 copy.42
  422.2 35.7 %all-reduce = (f32[2,192]{1,0:T(2,128)}, f32[768]{0:T(1024)}, f32[768]{0:T(1024)}, f32[768]{0:T(1024)}, f32[768]{0:T(1024)}, /*index=5*/f32[768]{0:T(1024)}, f32[768]{0:T(1024)}, f32[768]{0:T(1024)}, f32[4]{0:T(128)S(1)}) all-reduce(f32[2,192]{1,0:T(2,128)S(1)} %pad_maximum_fusion.5, ...), channel_id=1, replica_groups=mesh['shard'=4,'ctx'=2,'tp'=4] {'shard','ctx'}, use_global_device_ids=true, to_apply=%region_26.27 | all-reduce | flops 5764 | bytes 46112 | tf_op jit(solution)/shard_map/psum | solution.py:210
  459.7 5.2 all-reduce.12.cloned.1.call-done
  465.0 2.8 add_bitcast_fusion
  467.7 67.9 %reduce-scatter.19.cloned.1.call-done = f32[96,576]{1,0:T(8,128)} async-done(((f32[768,576]{1,0:T(8,128)}), f32[96,576]{1,0:T(8,128)}) %reduce-scatter.19.cloned.1.call-update) | async-done | bytes 221200
  537.5 70.1 %reduce-scatter.15.cloned.1.call-done = f32[96,768]{1,0:T(8,128)} async-done(((f32[768,768]{1,0:T(8,128)}), f32[96,768]{1,0:T(8,128)}) %reduce-scatter.15.cloned.1.call-update) | async-done | bytes 294928 | tf_op jit(solution)/shard_map/reduce_scatter | solution.py:197
  607.6 72.0 %reduce-scatter.17.cloned.1.call-done = f32[768,96]{0,1:T(8,128)} async-done(((f32[768,768]{0,1:T(8,128)}), f32[768,96]{0,1:T(8,128)}) %reduce-scatter.17.cloned.1.call-update) | async-done | bytes 294928 | tf_op jit(solution)/shard_map/reduce_scatter | solution.py:198
  (235 shorter events, 37.4 us)
Async XLA Ops:
  8.0 46.3 %copy-start.15 = (bf16[1,512,768]{2,1,0:T(8,128)(2,1)S(1)}, bf16[1,512,768]{2,1,0:T(8,128)(2,1)}, u32[]{:S(2)}) copy-start(bf16[1,512,768]{2,1,0:T(8,128)(2,1)} %param.16) | copy-start | bytes 2359300
  8.0 146.7 %all-reduce.6.cloned.1.call-start = ((), (), s32[]{:S(2)}) async-start(), calls=%async_computation.6 | async-start | bytes 3145728 | tf_op jit(solution)/shard_map/psum | solution.py:105
  14.1 95.0 %copy-start.63 = (pred[1024]{0:T(1024)(128)(4,1)}, pred[1024]{0:T(1024)(128)(4,1)S(1)}, u32[]{:S(2)}) copy-start(pred[1024]{0:T(1024)(128)(4,1)S(1)} %compare_reduce_fusion) | copy-start | bytes 3076
  14.1 95.0 %copy-start.45 = (s32[1,1,1024]{2,1,0:T(1,128)}, s32[1,1,1024]{2,1,0:T(1,128)S(1)}, u32[]{:S(2)}) copy-start(s32[1,1,1024]{2,1,0:T(1,128)S(1)} %slice.118) | copy-start | bytes 12292
  14.1 95.0 %copy-start.57 = (s32[512]{0:T(512)}, s32[512]{0:T(512)S(1)}, u32[]{:S(2)}) copy-start(s32[512]{0:T(512)S(1)} %iota_add_fusion) | copy-start | bytes 6148
  55.4 8.7 %copy-start.59 = (s32[1,512]{1,0:T(1,128)S(1)}, s32[1,512]{1,0:T(1,128)}, u32[]{:S(2)}) copy-start(s32[1,512]{1,0:T(1,128)} %param.17) | copy-start | bytes 6148
  55.6 13.1 %copy-start.29 = (bf16[1,512,192]{1,2,0:T(8,128)(2,1)}, bf16[1,512,192]{1,2,0:T(8,128)(2,1)S(1)}, u32[]{:S(2)}) copy-start(bf16[1,512,192]{1,2,0:T(8,128)(2,1)S(1)} %fusion.34) | copy-start | bytes 589828
  64.2 45.0 %copy-start.16 = (bf16[2,1,1024,192]{2,3,1,0:T(8,128)(2,1)}, bf16[2,1,1024,192]{2,3,1,0:T(8,128)(2,1)S(1)}, u32[]{:S(2)}) copy-start(bf16[2,1,1024,192]{2,3,1,0:T(8,128)(2,1)S(1)} %all_gather.24) | copy-start | bytes 2359300
  66.4 41.2 %copy-start.51 = (f32[512]{0:T(512)}, f32[512]{0:T(512)S(1)}, u32[]{:S(2)}) copy-start(f32[512]{0:T(512)S(1)} %get-tuple-element.107) | copy-start | bytes 6148
  68.6 40.6 %copy-start.52 = (f32[512]{0:T(512)}, f32[512]{0:T(512)S(1)}, u32[]{:S(2)}) copy-start(f32[512]{0:T(512)S(1)} %get-tuple-element.105) | copy-start | bytes 6148
  68.6 2.2 copy-start.38
  70.8 35.5 %copy-start.53 = (f32[512]{0:T(512)}, f32[512]{0:T(512)S(1)}, u32[]{:S(2)}) copy-start(f32[512]{0:T(512)S(1)} %get-tuple-element.103) | copy-start | bytes 6148
  102.1 4.3 copy-start.22
  106.3 2.8 copy-start.55
  107.6 3.1 copy-start.31
  110.7 44.0 %copy-start.47 = (f32[768]{0:T(1024)S(1)}, f32[768]{0:T(1024)}, u32[]{:S(2)}) copy-start(f32[768]{0:T(1024)} %param.22) | copy-start | bytes 9220
  112.3 44.5 %all-gather.3.cloned.1.call-start = ((), (), s32[]{:S(2)}) async-start(), calls=%async_computation.7 | async-start | bytes 1327104 | tf_op jit(solution)/shard_map/all_gather | solution.py:72
  112.9 84.9 %all-gather.5.cloned.1.call-start = ((), (), s32[]{:S(2)}) async-start(), calls=%async_computation.8 | async-start | bytes 1327104 | tf_op jit(solution)/shard_map/all_gather | solution.py:73
  113.5 129.8 %all-reduce.8.cloned.1.call-start = ((), (), s32[]{:S(2)}) async-start(), calls=%async_computation.9 | async-start | bytes 3145728 | tf_op jit(solution)/shard_map/psum | solution.py:113
  201.8 41.5 %copy-start.14 = (f32[512,768]{1,0:T(8,128)S(1)}, f32[512,768]{1,0:T(8,128)}, u32[]{:S(2)}) copy-start(f32[512,768]{1,0:T(8,128)} %all-reduce.6.cloned.1.call-done) | copy-start | bytes 4718596
  201.8 99.5 %all-reduce.10.cloned.1.call-start = ((), (), s32[]{:S(2)}) async-start(), calls=%async_computation.10 | async-start | bytes 3145728 | tf_op jit(solution)/shard_map/psum | solution.py:130
  249.5 2.4 copy-start.78
  251.1 4.3 copy-start.3
  251.1 2.1 copy-start.75
  251.1 4.3 copy-start.41
  251.9 3.5 copy-start.27
  253.2 3.1 copy-start.74
  258.3 77.0 %reduce-scatter.11.cloned.1.call-start = ((), (), s32[]{:S(2)}) async-start(), calls=%async_computation.11 | async-start | bytes 1179648 | tf_op jit(solution)/shard_map/reduce_scatter | solution.py:177
  305.3 2.7 copy-start.23
  307.5 2.0 copy-start.19
  312.4 2.7 copy-start.12
  315.7 2.2 copy-start.26
  317.6 37.3 %reduce-scatter.13.cloned.1.call-start = ((), (), s32[]{:S(2)}) async-start(), calls=%async_computation.12 | async-start | bytes 1179648 | tf_op jit(solution)/shard_map/reduce_scatter | solution.py:178
  317.9 2.2 copy-start.11
  323.0 97.5 %reduce-scatter.21.cloned.1.call-start = ((), (), s32[]{:S(2)}) async-start(), calls=%async_computation.17 | async-start | bytes 884736
  325.8 139.2 %all-reduce.12.cloned.1.call-start = ((), (), s32[]{:S(2)}) async-start(), calls=%async_computation.13 | async-start | bytes 3145728 | tf_op jit(solution)/shard_map/psum | solution.py:190
  325.8 3.4 copy-start.7
  360.7 174.9 %reduce-scatter.19.cloned.1.call-start = ((), (), s32[]{:S(2)}) async-start(), calls=%async_computation.16 | async-start | bytes 2211840
  372.8 234.8 %reduce-scatter.15.cloned.1.call-start = ((), (), s32[]{:S(2)}) async-start(), calls=%async_computation.14 | async-start | bytes 2654208 | tf_op jit(solution)/shard_map/reduce_scatter | solution.py:197
  377.0 302.6 %reduce-scatter.17.cloned.1.call-start = ((), (), s32[]{:S(2)}) async-start(), calls=%async_computation.15 | async-start | bytes 2654208 | tf_op jit(solution)/shard_map/reduce_scatter | solution.py:198
  382.0 40.2 %copy-start.65 = (f32[192]{0:T(256)S(1)}, f32[192]{0:T(256)}, u32[]{:S(2)}) copy-start(f32[192]{0:T(256)} %get-tuple-element.71) | copy-start | bytes 2308
  382.0 40.2 %copy-start.42 = (f32[768]{0:T(1024)S(1)}, f32[768]{0:T(1024)}, u32[]{:S(2)}) copy-start(f32[768]{0:T(1024)} %get-tuple-element.45) | copy-start | bytes 9220
  382.0 40.2 %copy-start.43 = (f32[768]{0:T(1024)S(1)}, f32[768]{0:T(1024)}, u32[]{:S(2)}) copy-start(f32[768]{0:T(1024)} %get-tuple-element.65) | copy-start | bytes 9220
  382.0 40.2 %copy-start.44 = (f32[768]{0:T(1024)S(1)}, f32[768]{0:T(1024)}, u32[]{:S(2)}) copy-start(f32[768]{0:T(1024)} %get-tuple-element.69) | copy-start | bytes 9220
  382.1 40.2 %copy-start.49 = (f32[768]{0:T(1024)S(1)}, f32[768]{0:T(1024)}, u32[]{:S(2)}) copy-start(f32[768]{0:T(1024)} %get-tuple-element.47) | copy-start | bytes 9220
  382.1 40.2 %copy-start.50 = (f32[768]{0:T(1024)S(1)}, f32[768]{0:T(1024)}, u32[]{:S(2)}) copy-start(f32[768]{0:T(1024)} %get-tuple-element.49) | copy-start | bytes 9220
  382.1 40.2 %copy-start.66 = (f32[768]{0:T(1024)S(1)}, f32[768]{0:T(1024)}, u32[]{:S(2)}) copy-start(f32[768]{0:T(1024)} %get-tuple-element.67) | copy-start | bytes 9220
  382.1 82.9 %copy-start.2 = (f32[512,768]{1,0:T(8,128)S(1)}, f32[512,768]{1,0:T(8,128)}, u32[]{:S(2)}) copy-start(f32[512,768]{1,0:T(8,128)} %copy-done.1) | copy-start | bytes 4718596
  (43 other events, 60.7 us)
Sparse Core Ops, SparseCore 0:
  112.5 42.2 all-reduce.5
  202.0 41.3 all-reduce.7
  258.4 42.8 all-reduce.9
  317.7 17.4 reduce-scatter.10
  337.4 17.4 reduce-scatter.12
  358.1 62.4 reduce-scatter.20
  423.0 41.8 all-reduce.11
  468.8 66.7 reduce-scatter.18
  539.7 67.8 reduce-scatter.14
  611.5 68.0 reduce-scatter.16
Sparse Core Ops, SparseCore 1:
  115.0 40.7 all-gather.2
  157.8 40.0 all-gather.4
where the time goes:
time: 688 us; the launch traced here: 687 us
  waiting for transfers between devices  433 us (63%)
  blocking collectives  119 us (17%)
  matrix products  53 us (8%)
  other arithmetic  34.3 us (5%)
  local copies, waits for them, and re-layouts  29.7 us (4%)
  between operations  17.2 us (2%)
    unnamed x14, waiting for transfers between devices  104 us
    reduce_scatter x1, waiting for transfers between devices, body(): lax.psum_scatter(g_down, ('shard', 'ctx'), scatter_dimension=1, tiled=True)  72 us
    reduce_scatter x1, waiting for transfers between devices, body(): lax.psum_scatter(g_in, ('shard', 'ctx'), scatter_dimension=0, tiled=True)  70.1 us
    psum x1, waiting for transfers between devices, body(): lax.psum(jnp.dot(context, w_out, preferred_element_type=jnp.float32), 'tp')  41.2 us
    psum x1, waiting for transfers between devices, body(): lax.psum(jnp.einsum('nf,df->nd', d_pre, w_in, preferred_element_type=jnp....  40.4 us
    psum x1, waiting for transfers between devices, body(): lax.psum(jnp.dot(act_low, w_down, preferred_element_type=jnp.float32), 'tp')  39.9 us
    all_gather x1, blocking collectives, body(): lax.all_gather(qkv_weight, ('shard', 'ctx'), axis=1, tiled=True)  38.3 us
    all_gather x1, waiting for transfers between devices, body(): lax.all_gather(down_weight, ('shard', 'ctx'), axis=1, tiled=True)  37.3 us
  transfers between devices with their start and end apart: 12, of which 11 were waited for; matrix products, arithmetic and copies ran while one was open for 8% of the time, Pallas kernels for 0%

commit v1 on v0

v1 whole, which is shorter than its diff:
```python
import functools

import jax
import jax.numpy as jnp
from jax import lax
from jax.experimental import pallas as pl
from jax.experimental.pallas import tpu as pltpu
from jax.sharding import PartitionSpec as P

HEAD_DIM = 64
LANES = 128
TP = 4
EPS = 1e-12
MASKED = -1e30
F32 = jnp.float32
BF16 = jnp.bfloat16
STOP = 99


def nt(left, right):
    return lax.dot_general(left, right, (((1,), (1,)), ((), ())), preferred_element_type=F32)


def nn(left, right):
    return lax.dot_general(left, right, (((1,), (0,)), ((), ())), preferred_element_type=F32)


def gelu_and_slope(pre):
    scale = 0.7978845608028654
    cube = 0.044715
    square = pre * pre
    tanh = jnp.tanh(scale * pre * (1.0 + cube * square))
    half = 0.5 * (1.0 + tanh)
    slope = half + 0.5 * pre * (1.0 - tanh * tanh) * (scale * (1.0 + 3.0 * cube * square))
    return pre * half, slope


def column_sum(rows):
    return jnp.sum(rows, axis=0, keepdims=True)


def norm_forward(rows):
    mean = jnp.mean(rows, axis=-1, keepdims=True)
    centred = rows - mean
    spread = jnp.mean(centred * centred, axis=-1, keepdims=True)
    inverse = lax.rsqrt(spread + EPS)
    return centred * inverse, inverse


def norm_backward(grad, unit, inverse, gain):
    scaled = grad * gain
    first = jnp.mean(scaled, axis=-1, keepdims=True)
    second = jnp.mean(scaled * unit, axis=-1, keepdims=True)
    return inverse * (scaled - first - unit * second)


class Net:
    def __init__(self, send_sems, recv_sems):
        self.send_sems, self.recv_sems, self.copies = send_sems, recv_sems, []

    def send(self, source, target, where):
        place = len(self.copies)
        copy = pltpu.make_async_remote_copy(
            src_ref=source,
            dst_ref=target,
            send_sem=self.send_sems.at[place],
            recv_sem=self.recv_sems.at[place],
            device_id=where,
            device_id_type=pl.DeviceIdType.MESH,
        )
        copy.start()
        self.copies.append(copy)
        return copy

    def finish(self):
        for copy in self.copies:
            copy.wait_send()


def layer_kernel(dims, *refs):
    shards, ctxs, wctx, piece, width, chunk, heads = dims
    quarter = piece // TP
    cols = heads * HEAD_DIM
    (x_ref, cot_ref, code_ref, wa_ref, wi_ref, wd_ref, vec_ref,
     lo_ref, tg_ref, ga_ref, gi_ref, gd_ref, small_ref,
     wa, wi, wd, xt, ht, dft, dat, code_all, bias, kv, kvt, qm, sbuf, pt, ott, mt, vcol, cot,
     hid, act, slope, dffn, dpre, datt, lobuf, tgbuf,
     r1s, r1r, r2s, r2r, gown, gxs, gxr, gzs, gzr, dkvs, dkvr, dkv0, dqt, dproj, dqp, ctxp, dom0, dom1,
     unit1, hidden, resid2, resid1, sa, sb,
     sa1, sa2, sac, sas, sbc, sbs,
     local_sem, send_sems, recv_sems) = refs
    me_s, me_c, me_t = lax.axis_index("shard"), lax.axis_index("ctx"), lax.axis_index("tp")
    t1 = me_t + 1 - 2 * (me_t % 2)
    t2 = (me_t + 2) % TP
    t3 = (t1 + 2) % TP
    wc = me_c if wctx > 1 else 0
    net = Net(send_sems, recv_sems)

    def shard_at(step):
        return (me_s + step) % shards

    def ctx_at(step):
        return (me_c + step) % ctxs

    barrier = pltpu.get_barrier_semaphore()
    peers = [{"tp": t1}, {"tp": t2}]
    peers += [{"ctx": ctx_at(e)} for e in range(1, ctxs)]
    peers += [{"shard": shard_at(d)} for d in range(1, shards)]
    for peer in peers:
        pl.semaphore_signal(barrier, inc=1, device_id=peer, device_id_type=pl.DeviceIdType.MESH)
    pl.semaphore_wait(barrier, len(peers))

    def gather_start(buf, own):
        along = [net.send(own, buf.at[me_s, wc], {"shard": shard_at(d)}) for d in range(1, shards)]
        across = [net.send(own, buf.at[me_s, wc], {"ctx": ctx_at(e)}) for e in range(1, wctx)]
        buf[me_s, wc] = own[...]
        return along, across

    def gather_forward(buf, state):
        along, across = state
        for d in range(1, shards):
            along[d - 1].wait_recv()
            source = buf.at[shard_at(shards - d), wc]
            across += [net.send(source, source, {"ctx": ctx_at(e)}) for e in range(1, wctx)]

    def gather_wait(state):
        for copy in state[1]:
            copy.wait_recv()

    def whole(buf):
        return buf[...].reshape(width, buf.shape[-1])

    def reduce_start(k, partial):
        r1s[k, 0] = partial(t3)
        first = net.send(r1s.at[k, 0], r1r.at[k, 0], {"tp": t1})
        r1s[k, 1] = partial(t1)
        second = net.send(r1s.at[k, 1], r1r.at[k, 1], {"tp": t1})
        part = partial(t2)
        first.wait_recv()
        r2s[k] = (part + r1r[k, 0]).astype(BF16)
        third = net.send(r2s.at[k], r2r.at[k], {"tp": t2})
        return second, third, partial(me_t)

    def reduce_end(k, state):
        second, third, part = state
        second.wait_recv()
        part = part + r1r[k, 1]
        third.wait_recv()
        return part + r2r[k].astype(F32)

    def spread_start(buf, value):
        buf[me_t] = value
        over = net.send(buf.at[me_t], buf.at[me_t], {"tp": t2})
        near = net.send(buf.at[me_t], buf.at[me_t], {"tp": t1})
        return over, near

    def spread_pass(buf, state):
        state[0].wait_recv()
        return net.send(buf.at[t2], buf.at[t2], {"tp": t1})

    def grad_send(k):
        out = []
        for d in list(range(1, shards)) + [0]:
            s = shard_at(d)
            out.append(net.send(gxs.at[k, s], gxr.at[k, s], {"ctx": ctx_at(1)}))
        return out

    def grad_pass(k, state):
        out = []
        for d in range(1, shards):
            s = shard_at(d)
            total = gown[k, s]
            if wctx > 1:
                state[d - 1].wait_recv()
                total = total + gxr[k, s].astype(F32)
            gzs[k, d - 1] = total.astype(BF16)
            out.append(net.send(gzs.at[k, d - 1], gzr.at[k, d - 1], {"shard": s}))
        return out

    def grad_end(k, state, passed, out_ref):
        total = gown[k, me_s]
        if wctx > 1:
            state[shards - 1].wait_recv()
            total = total + gxr[k, me_s].astype(F32)
        for d in range(1, shards):
            passed[d - 1].wait_recv()
            total = total + gzr[k, d - 1].astype(F32)
        out_ref[...] = total

    def grad_product(k, terms):
        for c in range(wctx - 1, -1, -1):
            where = (me_c + c) % wctx if wctx > 1 else 0
            done = {}
            for left, right, start in terms:
                value = nn(left[where].reshape(shards * chunk, piece), right)
                done[start] = done[start] + value if start in done else value
            for start, value in done.items():
                n = value.shape[1]
                value = value.reshape(shards, chunk, n)
                if c > 0:
                    gxs[k, :, :, start:start + n] = value.astype(BF16)
                else:
                    gown[k, :, :, start:start + n] = value

    def store_transposed(target, value):
        turned = jnp.transpose(value)
        for s in range(shards):
            for c in range(wctx):
                begin = (s * wctx + c) * chunk
                target[c, s] = turned[begin:begin + chunk]

    def exchange(buf, source, axis, at, count, me):
        buf[me] = source
        out = [net.send(buf.at[me], buf.at[me], {axis: at(e)}) for e in range(1, count)]
        return out

    def exchange_end(buf, state, count):
        for copy in state:
            copy.wait_recv()
        total = buf[0]
        for i in range(1, count):
            total = total + buf[i]
        return total

    a_state = gather_start(wa, wa_ref)
    code_all[0] = code_ref[...]
    code_sends = [net.send(code_ref, code_all.at[e], {"ctx": ctx_at(e)}) for e in range(1, ctxs)]
    own_rows = pl.ds(pl.multiple_of(me_t * quarter, quarter), quarter)
    fetch = pltpu.make_async_copy(cot_ref.at[own_rows], cot, local_sem)
    fetch.start()
    store_transposed(xt, x_ref[...])
    for copy in code_sends:
        copy.wait_recv()
    query_code = code_ref[1:2, :]
    for e in range(ctxs):
        key_code = jnp.transpose(jnp.broadcast_to(code_all[e][0:1, :], (LANES, piece)))[:, 0:1]
        allowed = key_code == query_code
        if e == 0:
            rows = lax.broadcasted_iota(jnp.int32, (piece, piece), 0)
            lanes = lax.broadcasted_iota(jnp.int32, (piece, piece), 1)
            allowed = allowed | (rows == lanes)
        bias[e] = jnp.where(allowed, 0.0, MASKED)
    valid_rows = jnp.transpose(jnp.broadcast_to(code_ref[2:3, :], (LANES, piece)))
    vcol[...] = valid_rows
    valid = vcol[own_rows, 0:1]
    gather_forward(wa, a_state)
    gather_wait(a_state)
    if STOP <= 1:
        fetch.wait()
        return net.finish()

    b_state = gather_start(wi, wi_ref)
    c_state = gather_start(wd, wd_ref)
    x = x_ref[...]
    w_all = whole(wa)
    kv[0] = (nn(x, w_all[:, 0:2 * cols]) + vec_ref[8:9, 0:2 * cols]).astype(BF16)
    kv_sends = [net.send(kv.at[0], kv.at[e], {"ctx": ctx_at(e)}) for e in range(1, ctxs)]
    q_pad = nn(x, w_all[:, 2 * cols:2 * cols + 256]) + vec_ref[7:8, 0:256]
    q_low = q_pad.astype(BF16).astype(F32) * 0.125
    lane = lax.broadcasted_iota(jnp.int32, (piece, 256), 1)
    for h in range(heads):
        inside = (lane >= h * HEAD_DIM) & (lane < (h + 1) * HEAD_DIM)
        qm[h] = jnp.where(inside, q_low, 0.0).astype(BF16)
    kvt[0] = jnp.transpose(kv[0])
    if STOP <= 2:
        fetch.wait()
        for c in b_state[0] + c_state[0] + b_state[1] + c_state[1] + kv_sends:
            c.wait_recv()
        return net.finish()

    tops = []
    for h in range(heads):
        s = nt(kv[0][:, 0:256], qm[h]) + bias[0]
        sbuf[h, 0] = s
        tops.append(jnp.max(s, axis=0, keepdims=True))
    gather_forward(wi, b_state)
    for e in range(1, ctxs):
        kv_sends[e - 1].wait_recv()
        kvt[e] = jnp.transpose(kv[e])
    ott[0:cols] = jnp.zeros((cols, piece), F32)
    mt[0:cols] = jnp.zeros((cols, piece), F32)
    for h in range(heads):
        top = tops[h]
        for e in range(1, ctxs):
            s = nt(kv[e][:, 0:256], qm[h]) + bias[e]
            sbuf[h, e] = s
            top = jnp.maximum(top, jnp.max(s, axis=0, keepdims=True))
        rows = slice(cols + h * HEAD_DIM, cols + (h + 1) * HEAD_DIM)
        total = jnp.zeros((1, piece), F32)
        mixed = jnp.zeros((HEAD_DIM, piece), F32)
        for e in range(ctxs):
            weights = jnp.exp(sbuf[h, e] - top)
            total = total + column_sum(weights)
            low = weights.astype(BF16)
            pt[h, e] = low
            mixed = mixed + nn(kvt[e, rows], low)
        inverse = 1.0 / total
        ott[rows] = mixed * inverse
        mt[rows] = jnp.broadcast_to(inverse, (HEAD_DIM, piece))
    ctxp[...] = jnp.transpose(ott[...]).astype(BF16)
    gather_forward(wd, c_state)
    if STOP <= 3:
        fetch.wait()
        gather_wait(b_state)
        gather_wait(c_state)
        return net.finish()

    def quarter_rows(q):
        return pl.ds(pl.multiple_of(q * quarter, quarter), quarter)

    state = reduce_start(0, lambda q: nt(ctxp[quarter_rows(q)], whole(wa)[:, 2 * cols:]))
    out_bias, gain1, shift1, in_bias = vec_ref[0:1], vec_ref[1:2], vec_ref[2:3], vec_ref[3:4]
    down_bias, gain2, shift2 = vec_ref[4:5], vec_ref[5:6], vec_ref[6:7]
    x_own = x_ref[own_rows].astype(F32)
    attn = reduce_end(0, state) + out_bias
    unit, inverse1 = norm_forward(x_own + attn)
    unit1[...] = unit
    own_hidden = unit * gain1 + shift1
    hidden[...] = own_hidden
    spread = spread_start(hid, own_hidden.astype(BF16))
    sa[6:7] = column_sum(valid * x_own * x_own)
    sa[7:8] = column_sum(valid * attn * attn)
    sa[9:10] = jnp.broadcast_to(column_sum(valid), (1, width))
    gather_wait(b_state)
    gather_wait(c_state)

    def expand(q):
        pre = nn(hid[q], whole(wi)) + in_bias
        a, s = gelu_and_slope(pre)
        act[q] = a.astype(BF16)
        slope[q] = s

    expand(me_t)
    spread[1].wait_recv()
    expand(t1)
    third = spread_pass(hid, spread)
    expand(t2)
    third.wait_recv()
    expand(t3)
    if STOP <= 4:
        fetch.wait()
        return net.finish()
    state = reduce_start(1, lambda q: nt(act[q], whole(wd)))
    store_transposed(ht, hid[...].reshape(piece, width))
    fetch.wait()
    ffn = reduce_end(1, state) + down_bias
    unit, inverse2 = norm_forward(hidden[...] + ffn)
    low_out = (unit * gain2 + shift2).astype(BF16)
    grad = cot[...]
    d_resid2 = norm_backward(grad, unit, inverse2, gain2)
    resid2[...] = d_resid2
    low = d_resid2.astype(BF16)
    spread = spread_start(dffn, low)
    spread_out = spread_start(lobuf, low_out)
    sa[8:9] = column_sum(valid * ffn * ffn)
    sa[3:4] = column_sum(low.astype(F32))
    sa[4:5] = column_sum(grad * unit)
    sa[5:6] = column_sum(grad)

    def expand_back(q):
        dpre[q] = (nn(dffn[q], whole(wd)) * slope[q]).astype(BF16)

    expand_back(me_t)
    spread[1].wait_recv()
    expand_back(t1)
    third = spread_pass(dffn, spread)
    expand_back(t2)
    third.wait_recv()
    expand_back(t3)
    third_out = spread_pass(lobuf, spread_out)
    state = reduce_start(2, lambda q: nt(dpre[q], whole(wi)))
    sb[0:1] = column_sum(dpre[...].reshape(piece, width).astype(F32))
    store_transposed(dft, dffn[...].reshape(piece, width))
    grad_product(2, [(dft, act[...].reshape(piece, width), 0)])
    d_state = grad_send(2) if wctx > 1 else None
    d_hidden = resid2[...] + reduce_end(2, state)
    d_resid1 = norm_backward(d_hidden, unit1[...], inverse1, gain1)
    resid1[...] = d_resid1
    low = d_resid1.astype(BF16)
    spread = spread_start(datt, low)
    sa[0:1] = column_sum(low.astype(F32))
    sa[1:2] = column_sum(d_hidden * unit1[...])
    sa[2:3] = column_sum(d_hidden)
    sa[10:16] = jnp.zeros((6, width), F32)
    near = net.send(sa, sa1, {"tp": t1})
    grad_product(1, [(ht, dpre[...].reshape(piece, width), 0)])
    i_state = grad_send(1) if wctx > 1 else None
    spread[1].wait_recv()
    third = spread_pass(datt, spread)
    d_pass = grad_pass(2, d_state)
    third.wait_recv()
    near.wait_recv()
    sa2[0] = sa[...] + sa1[...]
    over = net.send(sa2.at[0], sa2.at[1], {"tp": t2})
    if STOP <= 5:
        i_pass = grad_pass(1, i_state)
        grad_end(2, d_state, d_pass, gd_ref)
        grad_end(1, i_state, i_pass, gi_ref)
        over.wait_recv()
        spread_out[1].wait_recv()
        third_out.wait_recv()
        return net.finish()

    d_att_all = datt[...].reshape(piece, width)
    d_ctx = nn(d_att_all, whole(wa)[:, 2 * cols:]).astype(BF16).astype(F32)
    d_mix = d_ctx * jnp.transpose(mt[...])
    lane = lax.broadcasted_iota(jnp.int32, (piece, LANES), 1)
    dom0[...] = d_mix[:, 0:256].astype(BF16)
    last = d_mix[:, 256:384]
    dom1[0] = jnp.where(lane < HEAD_DIM, last, 0.0).astype(BF16)
    dom1[1] = jnp.where(lane >= HEAD_DIM, last, 0.0).astype(BF16)
    product = jnp.transpose(d_mix)[cols:] * ott[cols:]
    deltas = [column_sum(product[h * HEAD_DIM:(h + 1) * HEAD_DIM]) for h in range(heads)]
    i_pass = grad_pass(1, i_state)
    over.wait_recv()
    sa_c = exchange(sac, sa2[0] + sa2[1], "ctx", ctx_at, ctxs, me_c)
    dqt[...] = jnp.zeros((2 * cols, piece), F32)

    def attention_back(e):
        first = jnp.zeros((piece, 256), F32)
        second = jnp.zeros((piece, LANES), F32)
        for h in range(heads):
            if h == 0:
                d_probs = nt(kv[e][:, 0:256], dom0[...])
            else:
                d_probs = nt(kv[e][:, 256:384], dom1[h - 1])
            d_scores = (pt[h, e].astype(F32) * (d_probs - deltas[h])).astype(BF16)
            first = first + nn(d_scores, qm[h])
            if h == 0:
                first = first + nn(pt[h, e], dom0[...])
            else:
                second = second + nn(pt[h, e], dom1[h - 1])
            rows = slice(h * HEAD_DIM, (h + 1) * HEAD_DIM)
            dqt[rows] = dqt[rows] + nn(kvt[e, rows], d_scores)
        return first, second

    dkv_sends = []
    for e in range(ctxs - 1, 0, -1):
        first, second = attention_back(e)
        dkvs[e - 1, :, 0:256] = first.astype(BF16)
        dkvs[e - 1, :, 256:384] = second.astype(BF16)
        dkv_sends.append(net.send(dkvs.at[e - 1], dkvr.at[e - 1], {"ctx": ctx_at(ctxs - e)}))
    sa_s = exchange(sas, exchange_end(sac, sa_c, ctxs), "shard", shard_at, shards, me_s)
    first, second = attention_back(0)
    dkv0[:, 0:256] = first
    dkv0[:, 256:384] = second
    store_transposed(dat, d_att_all)
    total = dkv0[...]
    for i in range(ctxs - 1):
        dkv_sends[i].wait_recv()
        total = total + dkvr[ctxs - 2 - i].astype(F32)
    dproj[...] = total.astype(BF16)
    dqp[...] = jnp.transpose(dqt[...] * 0.125).astype(BF16)
    grad_product(0, [(xt, dproj[...], 0), (xt, dqp[...], 2 * cols), (dat, ctxp[...], 2 * cols)])
    a_gstate = grad_send(0) if wctx > 1 else None
    sb[1:2] = jnp.zeros((1, width), F32)
    sb[2:3] = jnp.zeros((1, width), F32)
    sb[1:2, 0:2 * cols] = column_sum(dproj[...].astype(F32))
    sb[2:3, 0:2 * cols] = column_sum(dqp[...].astype(F32))
    sb[3:8] = jnp.zeros((5, width), F32)
    sb_c = exchange(sbc, sb[...], "ctx", ctx_at, ctxs, me_c)

    def back_tokens(q):
        rows = quarter_rows(q)
        w = whole(wa)
        return nt(dproj[rows], w[:, 0:2 * cols]) + nt(dqp[rows, 0:256], w[:, 2 * cols:2 * cols + 256])

    state = reduce_start(3, back_tokens)
    sb_s = exchange(sbs, exchange_end(sbc, sb_c, ctxs), "shard", shard_at, shards, me_s)
    a_pass = grad_pass(0, a_gstate)
    spread = spread_start(tgbuf, (resid1[...] + reduce_end(3, state)).astype(BF16))
    grad_end(2, d_state, d_pass, gd_ref)
    grad_end(1, i_state, i_pass, gi_ref)
    spread_out[1].wait_recv()
    third_out.wait_recv()
    lo_ref[...] = lobuf[...]
    small_ref[0:16] = exchange_end(sas, sa_s, shards)
    third = spread_pass(tgbuf, spread)
    small_ref[16:24] = exchange_end(sbs, sb_s, shards)
    grad_end(0, a_gstate, a_pass, ga_ref)
    spread[1].wait_recv()
    third.wait_recv()
    tg_ref[...] = tgbuf[...]
    net.finish()


def run_layer(dims, copies, x, cot, code, wa, wi, wd, vec):
    shards, ctxs, wctx, piece, width, chunk, heads = dims
    quarter = piece // TP
    cols = heads * HEAD_DIM
    hidden_cols = wi.shape[1]
    vmem = pl.BlockSpec(memory_space=pltpu.VMEM)
    weights = (shards, wctx, chunk, width)
    turned = (wctx, shards, chunk, piece)
    V = pltpu.VMEM
    scratch = [
        V(weights, BF16), V(weights, BF16), V(weights, BF16),
        V(turned, BF16), V(turned, BF16), V(turned, BF16), V(turned, BF16),
        V((ctxs, 8, piece), F32), V((ctxs, piece, piece), F32),
        V((ctxs, piece, 2 * cols), BF16), V((ctxs, 2 * cols, piece), BF16), V((heads, piece, 256), BF16),
        V((heads, ctxs, piece, piece), F32), V((heads, ctxs, piece, piece), BF16),
        V((2 * cols, piece), F32), V((2 * cols, piece), F32), V((piece, LANES), F32), V((quarter, width), F32),
        V((TP, quarter, width), BF16), V((TP, quarter, hidden_cols), BF16), V((TP, quarter, hidden_cols), F32),
        V((TP, quarter, width), BF16), V((TP, quarter, hidden_cols), BF16), V((TP, quarter, width), BF16),
        V((TP, quarter, width), BF16), V((TP, quarter, width), BF16),
        V((4, 2, quarter, width), F32), V((4, 2, quarter, width), F32),
        V((4, quarter, width), BF16), V((4, quarter, width), BF16),
        V((3, shards, chunk, width), F32), V((3, shards, chunk, width), BF16), V((3, shards, chunk, width), BF16),
        V((3, max(shards - 1, 1), chunk, width), BF16), V((3, max(shards - 1, 1), chunk, width), BF16),
        V((ctxs - 1, piece, 2 * cols), BF16), V((ctxs - 1, piece, 2 * cols), BF16), V((piece, 2 * cols), F32),
        V((2 * cols, piece), F32), V((piece, 2 * cols), BF16), V((piece, 2 * cols), BF16), V((piece, 2 * cols), BF16),
        V((piece, 256), BF16), V((2, piece, LANES), BF16),
        V((quarter, width), F32), V((quarter, width), F32), V((quarter, width), F32), V((quarter, width), F32),
        V((16, width), F32), V((8, width), F32),
        V((16, width), F32), V((2, 16, width), F32), V((ctxs, 16, width), F32), V((shards, 16, width), F32),
        V((ctxs, 8, width), F32), V((shards, 8, width), F32),
        pltpu.SemaphoreType.DMA, pltpu.SemaphoreType.DMA((copies,)), pltpu.SemaphoreType.DMA((copies,)),
    ]
    return pl.pallas_call(
        functools.partial(layer_kernel, dims),
        out_shape=(
            jax.ShapeDtypeStruct((TP, quarter, width), BF16),
            jax.ShapeDtypeStruct((TP, quarter, width), BF16),
            jax.ShapeDtypeStruct((chunk, width), F32),
            jax.ShapeDtypeStruct((chunk, hidden_cols), F32),
            jax.ShapeDtypeStruct((chunk, hidden_cols), F32),
            jax.ShapeDtypeStruct((24, width), F32),
        ),
        in_specs=[vmem, pl.BlockSpec(memory_space=pl.ANY), vmem, vmem, vmem, vmem, vmem],
        out_specs=(vmem,) * 6,
        scratch_shapes=scratch,
        compiler_params=pltpu.CompilerParams(
            collective_id=0, has_side_effects=True, vmem_limit_bytes=67_043_328
        ),
        name="layer",
    )(x, cot, code, wa, wi, wd, vec)


def body(
    sizes,
    tokens, segment_ids, valid_mask, qkv_weight, qv_bias, out_weight, out_bias, norm1_gain, norm1_shift,
    in_weight, in_bias, down_weight, down_bias, norm2_gain, norm2_shift, out_cotangent,
):
    shards, ctxs = sizes
    _, piece, width = tokens.shape
    cols = qkv_weight.shape[2]
    heads = cols // HEAD_DIM
    own = jnp.concatenate([qkv_weight[1], qkv_weight[2], qkv_weight[0], out_weight.T], axis=1)
    parts = [own, in_weight, down_weight.T]
    wctx = ctxs
    if parts[0].shape[0] % 16 or ctxs > 2:
        wctx = 1
        parts = [lax.all_gather(part, "ctx", axis=0, tiled=True) for part in parts]
    chunk = parts[0].shape[0]
    dims = (shards, ctxs, wctx, piece, width, chunk, heads)
    seg = segment_ids.reshape(piece).astype(F32)
    valid = valid_mask.reshape(piece)
    zero = jnp.zeros((piece,), F32)
    code = jnp.stack([jnp.where(valid == 1, seg, -1.0), seg, valid.astype(F32), zero, zero, zero, zero, zero])
    q_bias = jnp.pad(qv_bias[0], (0, width - cols))
    kv_bias = jnp.pad(qv_bias[1], (cols, width - 2 * cols))
    none = jnp.zeros((width,), F32)
    vec = jnp.stack([out_bias, norm1_gain, norm1_shift, in_bias, down_bias, norm2_gain, norm2_shift,
                     q_bias, kv_bias] + [none] * 7)
    lo, tg, ga, gi, gd, small = run_layer(
        dims, 160, tokens.reshape(piece, width), out_cotangent.reshape(piece, width), code, *parts, vec
    )
    if wctx < ctxs:
        ga, gi, gd = (
            lax.psum_scatter(g, "ctx", scatter_dimension=0, tiled=True) for g in (ga, gi, gd)
        )
    g_qkv = jnp.stack([ga[:, 2 * cols:3 * cols], ga[:, 0:cols], ga[:, cols:2 * cols]])
    sums = jnp.sum(small[6:9], axis=1)
    stream_rms = jnp.sqrt(sums / (small[9, 0] * width))
    return (
        lo.reshape(1, piece, width),
        tg.reshape(1, piece, width).astype(F32),
        g_qkv,
        jnp.stack([small[18, 0:cols], small[17, cols:2 * cols]]),
        ga[:, 3 * cols:].T,
        small[0], small[1], small[2],
        gi,
        small[16],
        gd.T,
        small[3], small[4], small[5],
        stream_rms,
    )


def solution(mesh):
    sizes = (mesh.shape["shard"], mesh.shape["ctx"])
    return jax.shard_map(
        functools.partial(body, sizes),
        mesh=mesh,
        in_specs=(
            P("shard", "ctx", None), P("shard", "ctx"), P("shard", "ctx"),
            P(None, ("shard", "ctx"), "tp"), P(None, "tp"), P("tp", ("shard", "ctx")),
            P(), P(), P(),
            P(("shard", "ctx"), "tp"), P("tp"), P("tp", ("shard", "ctx")),
            P(), P(), P(),
            P("shard", "ctx", None),
        ),
        out_specs=(
            P("shard", "ctx", None), P("shard", "ctx", None),
            P(None, ("shard", "ctx"), "tp"), P(None, "tp"), P("tp", ("shard", "ctx")),
            P(), P(), P(),
            P(("shard", "ctx"), "tp"), P("tp"), P("tp", ("shard", "ctx")),
            P(), P(), P(), P(),
        ),
        check_vma=False,
    )
```

time: 688 us -> 186 us (0.27)
  waiting for transfers between devices: 433 us -> 0 us
  Pallas kernels: 0 us -> 159 us
  blocking collectives: 119 us -> 0 us
  matrix products: 53 us -> 0 us
  other arithmetic: 34.3 us -> 8.08 us
  between operations: 17.2 us -> 1.37 us
  local copies, waits for them, and re-layouts: 29.7 us -> 16.2 us
    reduce_scatter x4 -> x0, waiting for transfers between devices: 165 us -> none  [the longest x1 72 us: body(): lax.psum_scatter(g_down, ('shard', 'ctx'), scatter_dimension=1, tiled=True)]
    pallas_call x0 -> x1, Pallas kernels: none -> 159 us  [run_layer(): pl.pallas_call(functools.partial(layer_kernel, dims), out_shape=(jax.Shap...]
    psum x4 -> x0, waiting for transfers between devices: 127 us -> none  [the longest x1 41.2 us: body(): lax.psum(jnp.dot(context, w_out, preferred_element_type=jnp.float32), 'tp')]
    unnamed x14 -> x0, waiting for transfers between devices: 104 us -> none
    all_gather x4 -> x0, blocking collectives: 83.2 us -> none  [the longest x1 38.3 us: body(): lax.all_gather(qkv_weight, ('shard', 'ctx'), axis=1, tiled=True)]
    dot_general x29 -> x0, matrix products: 50.4 us -> none  [the longest x3 6.64 us: scaled_scores(): jnp.einsum('ae,be->ab', left, right, preferred_element_type=jnp.float32)]
    all_gather x2 -> x0, waiting for transfers between devices: 37.4 us -> none  [the longest x1 37.3 us: body(): lax.all_gather(down_weight, ('shard', 'ctx'), axis=1, tiled=True)]
    psum x1 -> x0, blocking collectives: 35.7 us -> none  [body(): lax.psum((d_qv_bias, d_out_bias, d_gain1, d_shift1, d_in_bias, d_down_bia...]
  transfers between devices with their start and end apart: 12 -> 0, of which waited for: 11 -> 0; matrix products, arithmetic and copies ran while one was open for 8% -> 0% of each run, Pallas kernels for 0% -> 0%
where the time goes in v1:
time: 186 us; the launch traced here: 184 us
  Pallas kernels  159 us (85%)
  local copies, waits for them, and re-layouts  16.2 us (9%)
  other arithmetic  8.08 us (4%)
    pallas_call x1, Pallas kernels, run_layer(): pl.pallas_call(functools.partial(layer_kernel, dims), out_shape=(jax.Shap...  159 us
    another operation x13, local copies, waits for them, and re-layouts, body(): jnp.stack([out_bias, norm1_gain, norm1_shift, in_bias, down_bias, norm2_g...  6.13 us
    unnamed x13, local copies, waits for them, and re-layouts  3.95 us

profile of v1, /device:TPU:0, one launch (start us, length us, event | category | flops | bytes accessed | tf_op | source)
XLA Modules:
  0.0 184.4 jit_solution(4887420233173704223)
XLA Ops:
  0.6 0.7 compare_select_fusion
  1.3 0.7 convert_element_type.27
  2.0 0.7 convert_element_type.28
  2.7 0.6 stack.61.refs_2_
  3.4 0.9 copy.31
  4.2 0.9 slice_bitcast_fusion.6
  5.1 0.8 pad_maximum_fusion.1.refs_3_
  5.9 0.7 stack.62
  6.6 0.7 stack.63
  7.3 0.7 stack.64
  7.9 0.7 stack.65
  8.6 0.7 stack.66
  9.3 0.7 stack.67
  10.0 0.7 stack.68
  10.7 0.8 fusion.1
  11.5 0.1 pad.9
  11.6 1.3 stack.73.refs_6_
  12.9 158.7 %layer.1 = (bf16[4,128,768]{2,1,0:T(8,128)(2,1)}, bf16[4,128,768]{2,1,0:T(8,128)(2,1)}, f32[96,768]{1,0:T(8,128)}, f32[96,768]{1,0:T(8,128)}, f32[96,768]{1,0:T(8,128)}, /*index=5*/f32[24,768]{1,0:T(8,128)}) custom-call(bf16[512,768]{1,0:T(8,128)(2,1)} %bitcast.29, f32[512,768]{1,0:T(8,128)} %bitcast.27, f32[8,512]{1,0:T(8,128)} %stack.61.refs_2_, ...), custom_call_target="tpu_custom_call" | custom-call | tf_op jit(solution)/shard_map/layer/pallas_call | solution.py:519
  171.6 0.0 copy-start.1
  171.6 0.0 copy-start
  171.6 2.5 %bitcast_convert_fusion = f32[1,512,768]{2,1,0:T(8,128)} fusion(bf16[1,512,768]{2,1,0:T(8,128)(2,1)} %bitcast.30), kind=kLoop, calls=%fused_computation | loop fusion | flops 393216 | bytes 2359296 | tf_op jit(solution)/shard_map/convert_element_type | solution.py:577
  174.1 0.0 copy-done.1
  174.1 0.0 copy-start.3
  174.1 0.1 slice_bitcast_fusion
  174.2 0.0 copy-start.2
  174.2 0.7 pad_maximum_fusion
  174.9 0.9 fusion
  175.8 0.6 pad_maximum_fusion.2
  176.4 0.7 copy.32
  177.1 1.6 slice_reduce_fusion.1
  178.7 0.9 slice_reduce_fusion
  179.7 1.2 slice.79
  181.5 0.5 divide_sqrt_fusion
  182.0 0.0 copy-done
  182.0 0.9 copy.36
  182.9 0.0 copy-done.3
  182.9 0.7 copy.37
  183.6 0.0 copy-done.2
  183.6 0.7 copy.38
  (8 shorter events, 0.0 us)
Async XLA Ops:
  171.6 2.5 %copy-start.1 = (f32[96,768]{1,0:T(8,128)S(1)}, f32[96,768]{1,0:T(8,128)}, u32[]{:S(2)}) copy-start(f32[96,768]{1,0:T(8,128)} %get-tuple-element.23) | copy-start | bytes 884740
  171.6 10.5 %copy-start = (bf16[4,128,768]{2,1,0:T(8,128)(2,1)S(1)}, bf16[4,128,768]{2,1,0:T(8,128)(2,1)}, u32[]{:S(2)}) copy-start(bf16[4,128,768]{2,1,0:T(8,128)(2,1)} %get-tuple-element.21) | copy-start | bytes 2359300
  174.1 8.9 %copy-start.3 = (f32[96,768]{1,0:T(8,128)S(1)}, f32[96,768]{1,0:T(8,128)}, u32[]{:S(2)}) copy-start(f32[96,768]{1,0:T(8,128)} %get-tuple-element.83) | copy-start | bytes 884740
  174.2 9.5 %copy-start.2 = (f32[96,768]{1,0:T(8,128)S(1)}, f32[96,768]{1,0:T(8,128)}, u32[]{:S(2)}) copy-start(f32[96,768]{1,0:T(8,128)} %get-tuple-element.26) | copy-start | bytes 884740

commit v2 on v1

--- a/solution.py
+++ b/solution.py
@@ -81,13 +81,15 @@
     shards, ctxs, wctx, piece, width, chunk, heads = dims
     quarter = piece // TP
     cols = heads * HEAD_DIM
-    (x_ref, cot_ref, code_ref, wa_ref, wi_ref, wd_ref, vec_ref,
+    (x_ref, cot_ref, seg_ref, valid_ref, qkv_ref, out_ref, wi_ref, wd_ref, qv_bias_ref, out_bias_ref, gain1_ref,
+     shift1_ref, in_bias_ref, down_bias_ref, gain2_ref, shift2_ref,
      lo_ref, tg_ref, ga_ref, gi_ref, gd_ref, small_ref,
      wa, wi, wd, xt, ht, dft, dat, code_all, bias, kv, kvt, qm, sbuf, pt, ott, mt, vcol, cot,
      hid, act, slope, dffn, dpre, datt, lobuf, tgbuf,
      r1s, r1r, r2s, r2r, gown, gxs, gxr, gzs, gzr, dkvs, dkvr, dkv0, dqt, dproj, dqp, ctxp, dom0, dom1,
      unit1, hidden, resid2, resid1, sa, sb,
      sa1, sa2, sac, sas, sbc, sbs,
+     wa_ref, code_ref, vec_ref,
      local_sem, send_sems, recv_sems) = refs
     me_s, me_c, me_t = lax.axis_index("shard"), lax.axis_index("ctx"), lax.axis_index("tp")
     t1 = me_t + 1 - 2 * (me_t % 2)
@@ -222,13 +224,29 @@
             total = total + buf[i]
         return total
 
+    if wctx < ctxs:
+        wa_ref[...] = qkv_ref[...]
+    else:
+        wa_ref[:, 0:cols] = qkv_ref[1]
+        wa_ref[:, cols:2 * cols] = qkv_ref[2]
+        wa_ref[:, 2 * cols:3 * cols] = qkv_ref[0]
+        wa_ref[:, 3 * cols:] = jnp.transpose(out_ref[...].astype(F32)).astype(BF16)
     a_state = gather_start(wa, wa_ref)
+    seg = seg_ref[...].astype(F32)
+    real = valid_ref[...] == 1
+    code_ref[...] = jnp.zeros_like(code_ref)
+    code_ref[0:1] = jnp.where(real, seg, -1.0)
+    code_ref[1:2] = seg
+    code_ref[2:3] = jnp.where(real, 1.0, 0.0)
     code_all[0] = code_ref[...]
     code_sends = [net.send(code_ref, code_all.at[e], {"ctx": ctx_at(e)}) for e in range(1, ctxs)]
     own_rows = pl.ds(pl.multiple_of(me_t * quarter, quarter), quarter)
     fetch = pltpu.make_async_copy(cot_ref.at[own_rows], cot, local_sem)
     fetch.start()
     store_transposed(xt, x_ref[...])
+    vec_ref[...] = jnp.zeros_like(vec_ref)
+    vec_ref[0:1, 0:cols] = qv_bias_ref[0:1]
+    vec_ref[1:2, cols:2 * cols] = qv_bias_ref[1:2]
     for copy in code_sends:
         copy.wait_recv()
     query_code = code_ref[1:2, :]
@@ -253,9 +271,9 @@
     c_state = gather_start(wd, wd_ref)
     x = x_ref[...]
     w_all = whole(wa)
-    kv[0] = (nn(x, w_all[:, 0:2 * cols]) + vec_ref[8:9, 0:2 * cols]).astype(BF16)
+    kv[0] = (nn(x, w_all[:, 0:2 * cols]) + vec_ref[1:2, 0:2 * cols]).astype(BF16)
     kv_sends = [net.send(kv.at[0], kv.at[e], {"ctx": ctx_at(e)}) for e in range(1, ctxs)]
-    q_pad = nn(x, w_all[:, 2 * cols:2 * cols + 256]) + vec_ref[7:8, 0:256]
+    q_pad = nn(x, w_all[:, 2 * cols:2 * cols + 256]) + vec_ref[0:1, 0:256]
     q_low = q_pad.astype(BF16).astype(F32) * 0.125
     lane = lax.broadcasted_iota(jnp.int32, (piece, 256), 1)
     for h in range(heads):
@@ -309,8 +327,10 @@
         return pl.ds(pl.multiple_of(q * quarter, quarter), quarter)
 
     state = reduce_start(0, lambda q: nt(ctxp[quarter_rows(q)], whole(wa)[:, 2 * cols:]))
-    out_bias, gain1, shift1, in_bias = vec_ref[0:1], vec_ref[1:2], vec_ref[2:3], vec_ref[3:4]
-    down_bias, gain2, shift2 = vec_ref[4:5], vec_ref[5:6], vec_ref[6:7]
+    out_bias, gain1, shift1, in_bias = (
+        ref[...].reshape(1, -1) for ref in (out_bias_ref, gain1_ref, shift1_ref, in_bias_ref)
+    )
+    down_bias, gain2, shift2 = (ref[...].reshape(1, -1) for ref in (down_bias_ref, gain2_ref, shift2_ref))
     x_own = x_ref[own_rows].astype(F32)
     attn = reduce_end(0, state) + out_bias
     unit, inverse1 = norm_forward(x_own + attn)
@@ -484,11 +504,11 @@
     net.finish()
 
 
-def run_layer(dims, copies, x, cot, code, wa, wi, wd, vec):
+def run_layer(dims, copies, *operands):
     shards, ctxs, wctx, piece, width, chunk, heads = dims
     quarter = piece // TP
     cols = heads * HEAD_DIM
-    hidden_cols = wi.shape[1]
+    hidden_cols = operands[6].shape[1]
     vmem = pl.BlockSpec(memory_space=pltpu.VMEM)
     weights = (shards, wctx, chunk, width)
     turned = (wctx, shards, chunk, piece)
@@ -514,6 +534,7 @@
         V((16, width), F32), V((8, width), F32),
         V((16, width), F32), V((2, 16, width), F32), V((ctxs, 16, width), F32), V((shards, 16, width), F32),
         V((ctxs, 8, width), F32), V((shards, 8, width), F32),
+        V((chunk, width), BF16), V((8, piece), F32), V((8, 2 * cols), F32),
         pltpu.SemaphoreType.DMA, pltpu.SemaphoreType.DMA((copies,)), pltpu.SemaphoreType.DMA((copies,)),
     ]
     return pl.pallas_call(
@@ -526,14 +547,53 @@
             jax.ShapeDtypeStruct((chunk, hidden_cols), F32),
             jax.ShapeDtypeStruct((24, width), F32),
         ),
-        in_specs=[vmem, pl.BlockSpec(memory_space=pl.ANY), vmem, vmem, vmem, vmem, vmem],
+        in_specs=[vmem, pl.BlockSpec(memory_space=pl.ANY)] + [vmem] * (len(operands) - 2),
         out_specs=(vmem,) * 6,
         scratch_shapes=scratch,
         compiler_params=pltpu.CompilerParams(
             collective_id=0, has_side_effects=True, vmem_limit_bytes=67_043_328
         ),
         name="layer",
-    )(x, cot, code, wa, wi, wd, vec)
+    )(*operands)
+
+
+def finish_kernel(cols, *refs):
+    (lo, tg, ga, gi, gd, small,
+     lo_out, tg_out, qkv_out, qv_out, out_out, in_out, down_out, v0, v1, v2, v3, v4, v5, v6, rms_out) = refs
+    lo_out[...] = lo[...]
+    tg_out[...] = tg[...].astype(F32)
+    qkv_out[0] = ga[:, 2 * cols:3 * cols]
+    qkv_out[1] = ga[:, 0:cols]
+    qkv_out[2] = ga[:, cols:2 * cols]
+    out_out[...] = jnp.transpose(ga[:, 3 * cols:])
+    in_out[...] = gi[...]
+    down_out[...] = gd[...]
+    qv_out[0:1] = small[18:19, 0:cols]
+    qv_out[1:2] = small[17:18, cols:2 * cols]
+    for row, ref in zip((0, 1, 2, 16, 3, 4, 5), (v0, v1, v2, v3, v4, v5, v6)):
+        ref[...] = small[row]
+    count = small[9:10, 0:1] * small.shape[1]
+    for i in range(3):
+        rms_out[0:1, i:i + 1] = jnp.sqrt(jnp.sum(small[6 + i:7 + i], axis=1, keepdims=True) / count)
+
+
+def run_finish(cols, *operands):
+    _, quarter, width = operands[0].shape
+    chunk, hidden_cols = operands[3].shape
+    shapes = [
+        ((TP, quarter, width), BF16), ((TP, quarter, width), F32), ((3, chunk, cols), F32), ((2, cols), F32),
+        ((cols, chunk), F32), ((chunk, hidden_cols), F32), ((chunk, hidden_cols), F32),
+        ((width,), F32), ((width,), F32), ((width,), F32), ((hidden_cols,), F32),
+        ((width,), F32), ((width,), F32), ((width,), F32), ((1, 3), F32),
+    ]
+    vmem = pl.BlockSpec(memory_space=pltpu.VMEM)
+    return pl.pallas_call(
+        functools.partial(finish_kernel, cols),
+        out_shape=tuple(jax.ShapeDtypeStruct(*shape) for shape in shapes),
+        in_specs=[vmem] * len(operands),
+        out_specs=(vmem,) * len(shapes),
+        name="finish",
+    )(*operands)
 
 
 def body(
@@ -545,33 +605,35 @@
     _, piece, width = tokens.shape
     cols = qkv_weight.shape[2]
     heads = cols // HEAD_DIM
-    own = jnp.concatenate([qkv_weight[1], qkv_weight[2], qkv_weight[0], out_weight.T], axis=1)
-    parts = [own, in_weight, down_weight.T]
-    wctx = ctxs
-    if parts[0].shape[0] % 16 or ctxs > 2:
+    raw = qkv_weight.shape[1] % 16 == 0 and ctxs <= 2
+    if raw:
+        wctx = ctxs
+        parts = [qkv_weight, out_weight, in_weight, down_weight.T]
+        chunk = in_weight.shape[0]
+    else:
         wctx = 1
-        parts = [lax.all_gather(part, "ctx", axis=0, tiled=True) for part in parts]
-    chunk = parts[0].shape[0]
+        own = jnp.concatenate([qkv_weight[1], qkv_weight[2], qkv_weight[0], out_weight.T], axis=1)
+        own, into, down = (
+            lax.all_gather(part, "ctx", axis=0, tiled=True) for part in (own, in_weight, down_weight.T)
+        )
+        parts = [own, out_weight, into, down]
+        chunk = own.shape[0]
     dims = (shards, ctxs, wctx, piece, width, chunk, heads)
-    seg = segment_ids.reshape(piece).astype(F32)
-    valid = valid_mask.reshape(piece)
-    zero = jnp.zeros((piece,), F32)
-    code = jnp.stack([jnp.where(valid == 1, seg, -1.0), seg, valid.astype(F32), zero, zero, zero, zero, zero])
-    q_bias = jnp.pad(qv_bias[0], (0, width - cols))
-    kv_bias = jnp.pad(qv_bias[1], (cols, width - 2 * cols))
-    none = jnp.zeros((width,), F32)
-    vec = jnp.stack([out_bias, norm1_gain, norm1_shift, in_bias, down_bias, norm2_gain, norm2_shift,
-                     q_bias, kv_bias] + [none] * 7)
-    lo, tg, ga, gi, gd, small = run_layer(
-        dims, 160, tokens.reshape(piece, width), out_cotangent.reshape(piece, width), code, *parts, vec
+    vectors = [out_bias, norm1_gain, norm1_shift, in_bias, down_bias, norm2_gain, norm2_shift]
+    results = run_layer(
+        dims, 160, tokens.reshape(piece, width), out_cotangent.reshape(piece, width), segment_ids, valid_mask,
+        *parts, qv_bias, *vectors
     )
-    if wctx < ctxs:
-        ga, gi, gd = (
-            lax.psum_scatter(g, "ctx", scatter_dimension=0, tiled=True) for g in (ga, gi, gd)
+    if raw:
+        lo, tg, g_qkv, g_qv, g_out, g_in, g_down, *sums, rms = run_finish(cols, *results)
+        return (
+            lo.reshape(1, piece, width), tg.reshape(1, piece, width), g_qkv, g_qv, g_out, sums[0], sums[1], sums[2],
+            g_in, sums[3], g_down.T, sums[4], sums[5], sums[6], rms.reshape(-1),
         )
+    lo, tg, ga, gi, gd, small = results
+    ga, gi, gd = (lax.psum_scatter(g, "ctx", scatter_dimension=0, tiled=True) for g in (ga, gi, gd))
     g_qkv = jnp.stack([ga[:, 2 * cols:3 * cols], ga[:, 0:cols], ga[:, cols:2 * cols]])
     sums = jnp.sum(small[6:9], axis=1)
-    stream_rms = jnp.sqrt(sums / (small[9, 0] * width))
     return (
         lo.reshape(1, piece, width),
         tg.reshape(1, piece, width).astype(F32),
@@ -583,7 +645,7 @@
         small[16],
         gd.T,
         small[3], small[4], small[5],
-        stream_rms,
+        jnp.sqrt(sums / (small[9, 0] * width)),
     )
 
 

time: 186 us -> 165 us (0.89)
  local copies, waits for them, and re-layouts: 16.2 us -> 0 us
  other arithmetic: 8.08 us -> 0 us
  Pallas kernels: 159 us -> 163 us
    another operation x16 -> x0, local copies, waits for them, and re-layouts: 6.76 us -> none  [the longest x13 6.13 us: body(): jnp.stack([out_bias, norm1_gain, norm1_shift, in_bias, down_bias, norm2_g...]
    slice x4 -> x0, local copies, waits for them, and re-layouts: 4.44 us -> none  [the longest x1 1.63 us: body(): small[5]]
    unnamed x13 -> x0, local copies, waits for them, and re-layouts: 3.95 us -> none
    convert_element_type x3 -> x0, other arithmetic: 3.84 us -> none  [the longest x1 2.47 us: body(): tg.reshape(1, piece, width).astype(F32)]
    pallas_call x0 -> x1, Pallas kernels: none -> 3.68 us  [run_finish(): pl.pallas_call(functools.partial(finish_kernel, cols), out_shape=tuple((j...]
where the time goes in v2:
time: 165 us; the launch traced here: 163 us
  Pallas kernels  163 us (99%)
    pallas_call x1, Pallas kernels, run_layer(): pl.pallas_call(functools.partial(layer_kernel, dims), out_shape=(jax.Shap...  159 us
    pallas_call x1, Pallas kernels, run_finish(): pl.pallas_call(functools.partial(finish_kernel, cols), out_shape=tuple((j...  3.68 us

profile of v2, /device:TPU:0, one launch (start us, length us, event | category | flops | bytes accessed | tf_op | source)
XLA Modules:
  0.0 163.5 jit_solution(4506769586413789341)
XLA Ops:
  0.7 159.0 %layer.1 = (bf16[4,128,768]{2,1,0:T(8,128)(2,1)}, bf16[4,128,768]{2,1,0:T(8,128)(2,1)}, f32[96,768]{1,0:T(8,128)}, f32[96,768]{1,0:T(8,128)}, f32[96,768]{1,0:T(8,128)}, /*index=5*/f32[24,768]{1,0:T(8,128)}) custom-call(bf16[512,768]{1,0:T(8,128)(2,1)} %bitcast.8, f32[512,768]{1,0:T(8,128)} %bitcast.7, s32[1,512]{1,0:T(1,128)} %refs_2_.1, s32[1,512]{1,0:T(1,128)} %refs_3_.1, ...), custom_call_target="tpu_custom_call" | custom-call | tf_op jit(solution)/shard_map/layer/pallas_call | solution.py:540
  159.7 3.7 %finish.1 = (bf16[4,128,768]{2,1,0:T(8,128)(2,1)}, f32[4,128,768]{2,1,0:T(8,128)}, f32[3,96,192]{2,1,0:T(8,128)}, f32[2,192]{1,0:T(2,128)}, f32[192,96]{1,0:T(8,...) custom-call(bf16[4,128,768]{2,1,0:T(8,128)(2,1)} %get-tuple-element., ...), custom_call_target="tpu_custom_call" | custom-call | tf_op jit(solution)/shard_map/finish/pallas_call | solution.py:590

commit v3 on v2

v3 whole, which is shorter than its diff:
```python
import functools

import jax
import jax.numpy as jnp
from jax import lax
from jax.experimental import pallas as pl
from jax.experimental.pallas import tpu as pltpu
from jax.sharding import PartitionSpec as P

HEAD_DIM = 64
LANES = 128
TP = 4
EPS = 1e-12
MASKED = -1e30
F32 = jnp.float32
BF16 = jnp.bfloat16
BLOCKS = 4
ORDER = (
    "A0A1A2A3B0B1B2B3C0D0C1C2E0D1D2E1F0E2C3G0D3H0F1E3",
    "F2G1G2H1I0F3H2G3I1H3X0I2I3X1",
)


def nt(left, right):
    return lax.dot_general(left, right, (((1,), (1,)), ((), ())), preferred_element_type=F32)


def nn(left, right):
    return lax.dot_general(left, right, (((1,), (0,)), ((), ())), preferred_element_type=F32)


def gelu_and_slope(pre):
    scale = 0.7978845608028654
    cube = 0.044715
    square = pre * pre
    tanh = jnp.tanh(scale * pre * (1.0 + cube * square))
    half = 0.5 * (1.0 + tanh)
    slope = half + 0.5 * pre * (1.0 - tanh * tanh) * (scale * (1.0 + 3.0 * cube * square))
    return pre * half, slope


def column_sum(rows):
    return jnp.sum(rows, axis=0, keepdims=True)


def norm_forward(rows):
    mean = jnp.mean(rows, axis=-1, keepdims=True)
    centred = rows - mean
    spread = jnp.mean(centred * centred, axis=-1, keepdims=True)
    inverse = lax.rsqrt(spread + EPS)
    return centred * inverse, inverse


def norm_backward(grad, unit, inverse, gain):
    scaled = grad * gain
    first = jnp.mean(scaled, axis=-1, keepdims=True)
    second = jnp.mean(scaled * unit, axis=-1, keepdims=True)
    return inverse * (scaled - first - unit * second)


class Net:
    def __init__(self, send_sems, recv_sems):
        self.send_sems, self.recv_sems, self.copies = send_sems, recv_sems, []

    def send(self, source, target, where):
        place = len(self.copies)
        copy = pltpu.make_async_remote_copy(
            src_ref=source,
            dst_ref=target,
            send_sem=self.send_sems.at[place],
            recv_sem=self.recv_sems.at[place],
            device_id=where,
            device_id_type=pl.DeviceIdType.MESH,
        )
        copy.start()
        self.copies.append(copy)
        return copy

    def finish(self):
        for copy in self.copies:
            copy.wait_send()


def layer_kernel(dims, *refs):
    shards, ctxs, wctx, piece, width, chunk, heads = dims
    rows_b = piece // BLOCKS
    half = rows_b // 2
    cols = heads * HEAD_DIM
    (x_ref, cot_ref, seg_ref, valid_ref, qkv_ref, out_ref, wi_ref, wd_ref, qv_bias_ref, out_bias_ref, gain1_ref,
     shift1_ref, in_bias_ref, down_bias_ref, gain2_ref, shift2_ref,
     lo_ref, tg_ref, ga_ref, gi_ref, gd_ref, small_ref,
     wa, wi, wd, xt, ht, dft, dat, code_all, bias, kv, kvt, qm, sbuf, pt, ott, mt, vcol, cot,
     hid, act, slope, dffn, dpre, datt, lobuf, tgbuf,
     part, near_in, far_out, far_in, gown, gxs, gxr, gzs, gzr, dkvs, dkvr, dkv0, dqt, dproj, dqp, ctxp, dom0, dom1,
     unit1, hidden, resid2, resid1, sa, sb,
     sa1, sac, sas, sbc, sbs,
     wa_ref, code_ref, vec_ref,
     local_sems, send_sems, recv_sems) = refs
    me_s, me_c, me_t = lax.axis_index("shard"), lax.axis_index("ctx"), lax.axis_index("tp")
    mine = me_t % 2
    other = 1 - mine
    near = {"tp": me_t + 1 - 2 * mine}
    far = {"tp": (me_t + 2) % TP}
    wc = me_c if wctx > 1 else 0
    net = Net(send_sems, recv_sems)

    def shard_at(step):
        return (me_s + step) % shards

    def ctx_at(step):
        return (me_c + step) % ctxs

    steps = [d for d in range(1, shards) if d % 2] + [d for d in range(1, shards) if d % 2 == 0]

    barrier = pltpu.get_barrier_semaphore()
    peers = [near, far]
    peers += [{"ctx": ctx_at(e)} for e in range(1, ctxs)]
    peers += [{"shard": shard_at(d)} for d in range(1, shards)]
    for peer in peers:
        pl.semaphore_signal(barrier, inc=1, device_id=peer, device_id_type=pl.DeviceIdType.MESH)
    if wctx < ctxs:
        wa_ref[...] = qkv_ref[...]
    else:
        wa_ref[:, 0:cols] = qkv_ref[1]
        wa_ref[:, cols:2 * cols] = qkv_ref[2]
        wa_ref[:, 2 * cols:3 * cols] = qkv_ref[0]
        wa_ref[:, 3 * cols:] = jnp.transpose(out_ref[...].astype(F32)).astype(BF16)
    pl.semaphore_wait(barrier, len(peers))

    def gather_along(buf, own, lo, hi):
        span = slice(lo, hi)
        return {
            d: net.send(own.at[:, span], buf.at[me_s, wc, :, span], {"shard": shard_at(d)}) for d in steps
        }

    def gather_across(buf, own, lo, hi):
        span = slice(lo, hi)
        return [
            net.send(own.at[:, span], buf.at[me_s, wc, :, span], {"ctx": ctx_at(e)}) for e in range(1, wctx)
        ]

    def gather_forward(buf, along, across, lo, hi, which=None):
        span = slice(lo, hi)
        for d in steps if which is None else which:
            along[d].wait_recv()
            source = buf.at[shard_at(shards - d), wc, :, span]
            across += [net.send(source, source, {"ctx": ctx_at(e)}) for e in range(1, wctx)]

    def wait_all(copies):
        for copy in copies:
            copy.wait_recv()

    def whole(buf, lo, hi):
        return buf[:, :, :, lo:hi].reshape(width, hi - lo)

    def sum_start(k, b, value):
        part[k, b] = value.reshape(2, half, width)
        return net.send(part.at[k, b, other], near_in.at[k, b], near)

    def sum_pass(k, b, copy):
        copy.wait_recv()
        far_out[k, b] = (part[k, b, mine] + near_in[k, b]).astype(BF16)
        return net.send(far_out.at[k, b], far_in.at[k, b], far)

    def sum_end(k, b, copy):
        copy.wait_recv()
        return far_out[k, b].astype(F32) + far_in[k, b].astype(F32)

    def share(buf, b, value):
        buf[b, mine] = value
        return net.send(buf.at[b, mine], buf.at[b, mine], near)

    def block(b):
        return slice(b * rows_b, (b + 1) * rows_b)

    def own_rows(b):
        return pl.ds(pl.multiple_of(b * rows_b + mine * half, half), half)

    def grad_across(k, lo, hi):
        span = slice(lo, hi)
        if wctx == 1:
            return None
        return {
            d: net.send(gxs.at[k, shard_at(d), :, span], gxr.at[k, shard_at(d), :, span], {"ctx": ctx_at(1)})
            for d in steps + [0]
        }

    def grad_along(k, lo, hi, across):
        span = slice(lo, hi)
        out = {}
        for d in steps:
            s = shard_at(d)
            total = gown[k, s, :, span]
            if wctx > 1:
                across[d].wait_recv()
                total = total + gxr[k, s, :, span].astype(F32)
            gzs[k, d - 1, :, span] = total.astype(BF16)
            out[d] = net.send(gzs.at[k, d - 1, :, span], gzr.at[k, d - 1, :, span], {"shard": s})
        return out

    def grad_end(k, lo, hi, across, along, out_ref):
        span = slice(lo, hi)
        total = gown[k, me_s, :, span]
        if wctx > 1:
            across[0].wait_recv()
            total = total + gxr[k, me_s, :, span].astype(F32)
        for d in steps:
            along[d].wait_recv()
            total = total + gzr[k, d - 1, :, span].astype(F32)
        out_ref[:, span] = total

    def grad_product(k, lo, terms):
        for c in range(wctx - 1, -1, -1):
            where = (me_c + c) % wctx if wctx > 1 else 0
            value = 0.0
            for left, right in terms:
                value = value + nn(left[where].reshape(shards * chunk, piece), right)
            n = value.shape[1]
            value = value.reshape(shards, chunk, n)
            if c > 0:
                gxs[k, :, :, lo:lo + n] = value.astype(BF16)
            else:
                gown[k, :, :, lo:lo + n] = value

    def store_transposed(target, value):
        turned = jnp.transpose(value)
        for s in range(shards):
            for c in range(wctx):
                begin = (s * wctx + c) * chunk
                target[c, s] = turned[begin:begin + chunk]

    def exchange(buf, source, axis, at, count, me):
        buf[me] = source
        return [net.send(buf.at[me], buf.at[me], {axis: at(e)}) for e in range(1, count)]

    def exchange_end(buf, state, count):
        wait_all(state)
        total = buf[0]
        for i in range(1, count):
            total = total + buf[i]
        return total

    split = 2 * cols
    kv_along = gather_along(wa, wa_ref, 0, split)
    kv_across = gather_across(wa, wa_ref, 0, split)
    seg = seg_ref[...].astype(F32)
    real = valid_ref[...] == 1
    code_ref[...] = jnp.zeros_like(code_ref)
    code_ref[0:1] = jnp.where(real, seg, -1.0)
    code_ref[1:2] = seg
    code_ref[2:3] = jnp.where(real, 1.0, 0.0)
    code_sends = [net.send(code_ref, code_all.at[e], {"ctx": ctx_at(e)}) for e in range(1, ctxs)]
    qo_along = gather_along(wa, wa_ref, split, width)
    qo_across = gather_across(wa, wa_ref, split, width)
    wa[me_s, wc] = wa_ref[...]
    wi[me_s, wc] = wi_ref[...]
    wd[me_s, wc] = wd_ref[...]
    code_all[0] = code_ref[...]
    fetches = [
        pltpu.make_async_copy(cot_ref.at[own_rows(b)], cot.at[b], local_sems.at[b]) for b in range(BLOCKS)
    ]
    for fetch in fetches:
        fetch.start()
    vec_ref[...] = jnp.zeros_like(vec_ref)
    vec_ref[0:1, 0:cols] = qv_bias_ref[0:1]
    vec_ref[1:2, cols:2 * cols] = qv_bias_ref[1:2]
    vcol[...] = jnp.transpose(jnp.broadcast_to(code_ref[2:3, :], (LANES, piece)))
    gather_forward(wa, kv_along, kv_across, 0, split, steps[:1])
    query_code = code_ref[1:2, :]

    def store_bias(e):
        key_code = jnp.transpose(jnp.broadcast_to(code_all[e][0:1, :], (LANES, piece)))[:, 0:1]
        allowed = key_code == query_code
        if e == 0:
            rows = lax.broadcasted_iota(jnp.int32, (piece, piece), 0)
            lanes = lax.broadcasted_iota(jnp.int32, (piece, piece), 1)
            allowed = allowed | (rows == lanes)
        bias[e] = jnp.where(allowed, 0.0, MASKED)

    store_bias(0)
    gather_forward(wa, kv_along, kv_across, 0, split, steps[1:])
    gather_forward(wa, qo_along, qo_across, split, width, steps[:1])
    wait_all(kv_across)

    x = x_ref[...]
    kv[0] = (nn(x, whole(wa, 0, split)) + vec_ref[1:2, 0:split]).astype(BF16)
    gather_forward(wa, qo_along, qo_across, split, width, steps[1:])
    kv_sends = [net.send(kv.at[0], kv.at[e], {"ctx": ctx_at(e)}) for e in range(1, ctxs)]
    in_along = gather_along(wi, wi_ref, 0, width)
    down_along = gather_along(wd, wd_ref, 0, width)
    in_across = gather_across(wi, wi_ref, 0, width)
    down_across = gather_across(wd, wd_ref, 0, width)
    kvt[0] = jnp.transpose(kv[0])
    wait_all(code_sends)
    for e in range(1, ctxs):
        store_bias(e)
    wait_all(qo_across)
    q_low = (nn(x, whole(wa, split, split + 256)) + vec_ref[0:1, 0:256]).astype(BF16).astype(F32) * 0.125
    lane = lax.broadcasted_iota(jnp.int32, (piece, 256), 1)
    for h in range(heads):
        inside = (lane >= h * HEAD_DIM) & (lane < (h + 1) * HEAD_DIM)
        qm[h] = jnp.where(inside, q_low, 0.0).astype(BF16)

    tops = []
    for h in range(heads):
        s = nt(kv[0][:, 0:256], qm[h]) + bias[0]
        sbuf[h, 0] = s
        tops.append(jnp.max(s, axis=0, keepdims=True))
    store_transposed(xt, x_ref[...])
    ott[0:cols] = jnp.zeros((cols, piece), F32)
    mt[0:cols] = jnp.zeros((cols, piece), F32)
    gather_forward(wi, in_along, in_across, 0, width)
    for e in range(1, ctxs):
        kv_sends[e - 1].wait_recv()
        kvt[e] = jnp.transpose(kv[e])
    for h in range(heads):
        top = tops[h]
        for e in range(1, ctxs):
            s = nt(kv[e][:, 0:256], qm[h]) + bias[e]
            sbuf[h, e] = s
            top = jnp.maximum(top, jnp.max(s, axis=0, keepdims=True))
        rows = slice(cols + h * HEAD_DIM, cols + (h + 1) * HEAD_DIM)
        total = jnp.zeros((1, piece), F32)
        mixed = jnp.zeros((HEAD_DIM, piece), F32)
        for e in range(ctxs):
            weights = jnp.exp(sbuf[h, e] - top)
            total = total + column_sum(weights)
            low = weights.astype(BF16)
            pt[h, e] = low
            mixed = mixed + nn(kvt[e, rows], low)
        inverse = 1.0 / total
        ott[rows] = mixed * inverse
        mt[rows] = jnp.broadcast_to(inverse, (HEAD_DIM, piece))
    ctxp[...] = jnp.transpose(ott[...]).astype(BF16)

    out_bias, gain1, shift1, in_bias = (
        ref[...].reshape(1, -1) for ref in (out_bias_ref, gain1_ref, shift1_ref, in_bias_ref)
    )
    down_bias, gain2, shift2 = (ref[...].reshape(1, -1) for ref in (down_bias_ref, gain2_ref, shift2_ref))
    sa[...] = jnp.zeros_like(sa)
    near_copy, far_copy, share_copy, inverse1, out_copy = {}, {}, {}, {}, {}

    def add_sum(row, value):
        sa[row:row + 1] = sa[row:row + 1] + column_sum(value)

    def stage_a(b):
        near_copy[0, b] = sum_start(0, b, nt(ctxp[block(b)], whole(wa, split, width)))

    def stage_b(b):
        far_copy[0, b] = sum_pass(0, b, near_copy[0, b])

    def stage_c(b):
        attn = sum_end(0, b, far_copy[0, b]) + out_bias
        x_own = x_ref[own_rows(b)].astype(F32)
        valid = vcol[own_rows(b), 0:1]
        unit, inverse1[b] = norm_forward(x_own + attn)
        unit1[b] = unit
        own_hidden = unit * gain1 + shift1
        hidden[b] = own_hidden
        share_copy[0, b] = share(hid, b, own_hidden.astype(BF16))
        add_sum(6, valid * x_own * x_own)
        add_sum(7, valid * attn * attn)
        sa[9:10] = sa[9:10] + column_sum(valid)

    def stage_d(b):
        if b == 0:
            wait_all(in_across)
        share_copy[0, b].wait_recv()
        pre = nn(hid[b].reshape(rows_b, width), whole(wi, 0, width)) + in_bias
        value, slope[b] = gelu_and_slope(pre)
        act[b] = value.astype(BF16)
        if b == 0:
            gather_forward(wd, down_along, down_across, 0, width)
            wait_all(down_across)
        near_copy[1, b] = sum_start(1, b, nt(act[b], whole(wd, 0, width)))

    def stage_e(b):
        far_copy[1, b] = sum_pass(1, b, near_copy[1, b])

    def stage_f(b):
        if b == 0:
            for fetch in fetches:
                fetch.wait()
        ffn = sum_end(1, b, far_copy[1, b]) + down_bias
        valid = vcol[own_rows(b), 0:1]
        unit, inverse = norm_forward(hidden[b] + ffn)
        grad = cot[b]
        d_resid2 = norm_backward(grad, unit, inverse, gain2)
        low = d_resid2.astype(BF16)
        share_copy[1, b] = share(dffn, b, low)
        resid2[b] = d_resid2
        out_copy[b] = share(lobuf, b, (unit * gain2 + shift2).astype(BF16))
        add_sum(8, valid * ffn * ffn)
        add_sum(3, low.astype(F32))
        add_sum(4, grad * unit)
        add_sum(5, grad)

    def stage_g(b):
        share_copy[1, b].wait_recv()
        d_act = nn(dffn[b].reshape(rows_b, width), whole(wd, 0, width))
        dpre[b] = (d_act * slope[b]).astype(BF16)
        near_copy[2, b] = sum_start(2, b, nt(dpre[b], whole(wi, 0, width)))

    def stage_h(b):
        far_copy[2, b] = sum_pass(2, b, near_copy[2, b])

    def stage_i(b):
        d_hidden = resid2[b] + sum_end(2, b, far_copy[2, b])
        unit = unit1[b]
        d_resid1 = norm_backward(d_hidden, unit, inverse1[b], gain1)
        low = d_resid1.astype(BF16)
        share_copy[2, b] = share(datt, b, low)
        resid1[b] = d_resid1
        add_sum(0, low.astype(F32))
        add_sum(1, d_hidden * unit)
        add_sum(2, d_hidden)

    stages = dict(A=stage_a, B=stage_b, C=stage_c, D=stage_d, E=stage_e, F=stage_f, G=stage_g, H=stage_h, I=stage_i)
    state = {}

    def down_grads():
        store_transposed(dft, dffn[...].reshape(piece, width))
        grad_product(2, 0, [(dft, act[...].reshape(piece, width))])
        state["down"] = grad_across(2, 0, width)

    def in_grads():
        store_transposed(ht, hid[...].reshape(piece, width))
        grad_product(1, 0, [(ht, dpre[...].reshape(piece, width))])
        state["in"] = grad_across(1, 0, width)

    for name in ORDER:
        for i in range(0, len(name), 2):
            if name[i] == "X":
                (down_grads, in_grads)[int(name[i + 1])]()
            else:
                stages[name[i]](int(name[i + 1]))

    sb[...] = jnp.zeros_like(sb)
    sb[0:1] = column_sum(dpre[...].reshape(piece, width).astype(F32))
    sa_near = net.send(sa, sa1, near)
    down_sums = grad_along(2, 0, width, state["down"])
    for b in range(BLOCKS):
        share_copy[2, b].wait_recv()
    d_att_all = datt[...].reshape(piece, width)
    d_ctx = nn(d_att_all, whole(wa, split, width)).astype(BF16).astype(F32)
    d_mix = d_ctx * jnp.transpose(mt[...])
    lane = lax.broadcasted_iota(jnp.int32, (piece, LANES), 1)
    dom0[...] = d_mix[:, 0:256].astype(BF16)
    last = d_mix[:, 256:384]
    dom1[0] = jnp.where(lane < HEAD_DIM, last, 0.0).astype(BF16)
    dom1[1] = jnp.where(lane >= HEAD_DIM, last, 0.0).astype(BF16)
    product = jnp.transpose(d_mix)[cols:] * ott[cols:]
    deltas = [column_sum(product[h * HEAD_DIM:(h + 1) * HEAD_DIM]) for h in range(heads)]
    dqt[...] = jnp.zeros((2 * cols, piece), F32)

    def attention_back(e):
        first = jnp.zeros((piece, 256), F32)
        second = jnp.zeros((piece, LANES), F32)
        for h in range(heads):
            if h == 0:
                d_probs = nt(kv[e][:, 0:256], dom0[...])
            else:
                d_probs = nt(kv[e][:, 256:384], dom1[h - 1])
            d_scores = (pt[h, e].astype(F32) * (d_probs - deltas[h])).astype(BF16)
            first = first + nn(d_scores, qm[h])
            if h == 0:
                first = first + nn(pt[h, e], dom0[...])
            else:
                second = second + nn(pt[h, e], dom1[h - 1])
            rows = slice(h * HEAD_DIM, (h + 1) * HEAD_DIM)
            dqt[rows] = dqt[rows] + nn(kvt[e, rows], d_scores)
        return first, second

    dkv_sends = []
    for e in range(ctxs - 1, 0, -1):
        first, second = attention_back(e)
        dkvs[e - 1, :, 0:256] = first.astype(BF16)
        dkvs[e - 1, :, 256:384] = second.astype(BF16)
        dkv_sends.append(net.send(dkvs.at[e - 1], dkvr.at[e - 1], {"ctx": ctx_at(ctxs - e)}))
    sa_near.wait_recv()
    sa_c = exchange(sac, sa[...] + sa1[...], "ctx", ctx_at, ctxs, me_c)
    first, second = attention_back(0)
    dkv0[:, 0:256] = first
    dkv0[:, 256:384] = second
    dqp[...] = jnp.transpose(dqt[...] * 0.125).astype(BF16)
    store_transposed(dat, d_att_all)
    grad_product(0, split, [(xt, dqp[...]), (dat, ctxp[...])])
    qo_state = grad_across(0, split, width)
    in_sums = grad_along(1, 0, width, state["in"])
    sa_s = exchange(sas, exchange_end(sac, sa_c, ctxs), "shard", shard_at, shards, me_s)
    total = dkv0[...]
    for i in range(ctxs - 1):
        dkv_sends[i].wait_recv()
        total = total + dkvr[ctxs - 2 - i].astype(F32)
    dproj[...] = total.astype(BF16)

    def back_tokens(b):
        value = nt(dproj[block(b)], whole(wa, 0, split))
        return value + nt(dqp[block(b), 0:256], whole(wa, split, split + 256))

    for b in range(2):
        near_copy[3, b] = sum_start(3, b, back_tokens(b))
    far_copy[3, 0] = sum_pass(3, 0, near_copy[3, 0])
    grad_product(0, 0, [(xt, dproj[...])])
    kv_state = grad_across(0, 0, split)
    far_copy[3, 1] = sum_pass(3, 1, near_copy[3, 1])
    for b in range(2, BLOCKS):
        near_copy[3, b] = sum_start(3, b, back_tokens(b))
    for b in range(2, BLOCKS):
        far_copy[3, b] = sum_pass(3, b, near_copy[3, b])
    sb[1:2, 0:split] = column_sum(dproj[...].astype(F32))
    sb[2:3, 0:split] = column_sum(dqp[...].astype(F32))
    sb_c = exchange(sbc, sb[...], "ctx", ctx_at, ctxs, me_c)
    qo_sums = grad_along(0, split, width, qo_state)
    for b in range(BLOCKS):
        share_copy[3, b] = share(tgbuf, b, (resid1[b] + sum_end(3, b, far_copy[3, b])).astype(BF16))
    sb_s = exchange(sbs, exchange_end(sbc, sb_c, ctxs), "shard", shard_at, shards, me_s)
    kv_sums = grad_along(0, 0, split, kv_state)
    grad_end(2, 0, width, state["down"], down_sums, gd_ref)
    for b in range(BLOCKS):
        out_copy[b].wait_recv()
        lo_ref[b] = lobuf[b].reshape(rows_b, width)
    small_ref[0:16] = exchange_end(sas, sa_s, shards)
    grad_end(1, 0, width, state["in"], in_sums, gi_ref)
    for b in range(BLOCKS):
        share_copy[3, b].wait_recv()
        tg_ref[b] = tgbuf[b].reshape(rows_b, width)
    small_ref[16:24] = exchange_end(sbs, sb_s, shards)
    grad_end(0, split, width, qo_state, qo_sums, ga_ref)
    grad_end(0, 0, split, kv_state, kv_sums, ga_ref)
    net.finish()


def run_layer(dims, copies, *operands):
    shards, ctxs, wctx, piece, width, chunk, heads = dims
    rows_b = piece // BLOCKS
    half = rows_b // 2
    cols = heads * HEAD_DIM
    hidden_cols = operands[6].shape[1]
    vmem = pl.BlockSpec(memory_space=pltpu.VMEM)
    weights = (shards, wctx, chunk, width)
    turned = (wctx, shards, chunk, piece)
    V = pltpu.VMEM
    others = max(shards - 1, 1)
    shared = (BLOCKS, 2, half, width)
    hidden = (BLOCKS, rows_b, hidden_cols)
    scratch = [
        V(weights, BF16), V(weights, BF16), V(weights, BF16),
        V(turned, BF16), V(turned, BF16), V(turned, BF16), V(turned, BF16),
        V((ctxs, 8, piece), F32), V((ctxs, piece, piece), F32),
        V((ctxs, piece, 2 * cols), BF16), V((ctxs, 2 * cols, piece), BF16), V((heads, piece, 256), BF16),
        V((heads, ctxs, piece, piece), F32), V((heads, ctxs, piece, piece), BF16),
        V((2 * cols, piece), F32), V((2 * cols, piece), F32), V((piece, LANES), F32), V((BLOCKS, half, width), F32),
        V(shared, BF16), V(hidden, BF16), V(hidden, F32),
        V(shared, BF16), V(hidden, BF16), V(shared, BF16), V(shared, BF16), V(shared, BF16),
        V((4, BLOCKS, 2, half, width), F32), V((4, BLOCKS, half, width), F32),
        V((4, BLOCKS, half, width), BF16), V((4, BLOCKS, half, width), BF16),
        V((3, shards, chunk, width), F32), V((3, shards, chunk, width), BF16), V((3, shards, chunk, width), BF16),
        V((3, others, chunk, width), BF16), V((3, others, chunk, width), BF16),
        V((ctxs - 1, piece, 2 * cols), BF16), V((ctxs - 1, piece, 2 * cols), BF16), V((piece, 2 * cols), F32),
        V((2 * cols, piece), F32), V((piece, 2 * cols), BF16), V((piece, 2 * cols), BF16), V((piece, 2 * cols), BF16),
        V((piece, 256), BF16), V((2, piece, LANES), BF16),
        V((BLOCKS, half, width), F32), V((BLOCKS, half, width), F32), V((BLOCKS, half, width), F32),
        V((BLOCKS, half, width), F32),
        V((16, width), F32), V((8, width), F32),
        V((16, width), F32), V((ctxs, 16, width), F32), V((shards, 16, width), F32),
        V((ctxs, 8, width), F32), V((shards, 8, width), F32),
        V((chunk, width), BF16), V((8, piece), F32), V((8, 2 * cols), F32),
        pltpu.SemaphoreType.DMA((BLOCKS,)), pltpu.SemaphoreType.DMA((copies,)), pltpu.SemaphoreType.DMA((copies,)),
    ]
    return pl.pallas_call(
        functools.partial(layer_kernel, dims),
        out_shape=(
            jax.ShapeDtypeStruct((BLOCKS, rows_b, width), BF16),
            jax.ShapeDtypeStruct((BLOCKS, rows_b, width), BF16),
            jax.ShapeDtypeStruct((chunk, width), F32),
            jax.ShapeDtypeStruct((chunk, hidden_cols), F32),
            jax.ShapeDtypeStruct((chunk, hidden_cols), F32),
            jax.ShapeDtypeStruct((24, width), F32),
        ),
        in_specs=[vmem, pl.BlockSpec(memory_space=pl.ANY)] + [vmem] * (len(operands) - 2),
        out_specs=(vmem,) * 6,
        scratch_shapes=scratch,
        compiler_params=pltpu.CompilerParams(
            collective_id=0, has_side_effects=True, vmem_limit_bytes=67_043_328
        ),
        name="layer",
    )(*operands)


def finish_kernel(cols, *refs):
    (lo, tg, ga, gi, gd, small,
     lo_out, tg_out, qkv_out, qv_out, out_out, in_out, down_out, v0, v1, v2, v3, v4, v5, v6, rms_out) = refs
    lo_out[...] = lo[...]
    tg_out[...] = tg[...].astype(F32)
    qkv_out[0] = ga[:, 2 * cols:3 * cols]
    qkv_out[1] = ga[:, 0:cols]
    qkv_out[2] = ga[:, cols:2 * cols]
    out_out[...] = jnp.transpose(ga[:, 3 * cols:])
    in_out[...] = gi[...]
    down_out[...] = gd[...]
    qv_out[0:1] = small[18:19, 0:cols]
    qv_out[1:2] = small[17:18, cols:2 * cols]
    for row, ref in zip((0, 1, 2, 16, 3, 4, 5), (v0, v1, v2, v3, v4, v5, v6)):
        ref[...] = small[row]
    count = small[9:10, 0:1] * small.shape[1]
    for i in range(3):
        rms_out[0:1, i:i + 1] = jnp.sqrt(jnp.sum(small[6 + i:7 + i], axis=1, keepdims=True) / count)


def run_finish(cols, *operands):
    _, rows_b, width = operands[0].shape
    chunk, hidden_cols = operands[3].shape
    shapes = [
        ((BLOCKS, rows_b, width), BF16), ((BLOCKS, rows_b, width), F32), ((3, chunk, cols), F32), ((2, cols), F32),
        ((cols, chunk), F32), ((chunk, hidden_cols), F32), ((chunk, hidden_cols), F32),
        ((width,), F32), ((width,), F32), ((width,), F32), ((hidden_cols,), F32),
        ((width,), F32), ((width,), F32), ((width,), F32), ((1, 3), F32),
    ]
    vmem = pl.BlockSpec(memory_space=pltpu.VMEM)
    return pl.pallas_call(
        functools.partial(finish_kernel, cols),
        out_shape=tuple(jax.ShapeDtypeStruct(*shape) for shape in shapes),
        in_specs=[vmem] * len(operands),
        out_specs=(vmem,) * len(shapes),
        name="finish",
    )(*operands)


def body(
    sizes,
    tokens, segment_ids, valid_mask, qkv_weight, qv_bias, out_weight, out_bias, norm1_gain, norm1_shift,
    in_weight, in_bias, down_weight, down_bias, norm2_gain, norm2_shift, out_cotangent,
):
    shards, ctxs = sizes
    _, piece, width = tokens.shape
    cols = qkv_weight.shape[2]
    heads = cols // HEAD_DIM
    raw = qkv_weight.shape[1] % 16 == 0 and ctxs <= 2
    if raw:
        wctx = ctxs
        parts = [qkv_weight, out_weight, in_weight, down_weight.T]
        chunk = in_weight.shape[0]
    else:
        wctx = 1
        own = jnp.concatenate([qkv_weight[1], qkv_weight[2], qkv_weight[0], out_weight.T], axis=1)
        own, into, down = (
            lax.all_gather(part, "ctx", axis=0, tiled=True) for part in (own, in_weight, down_weight.T)
        )
        parts = [own, out_weight, into, down]
        chunk = own.shape[0]
    dims = (shards, ctxs, wctx, piece, width, chunk, heads)
    vectors = [out_bias, norm1_gain, norm1_shift, in_bias, down_bias, norm2_gain, norm2_shift]
    results = run_layer(
        dims, 160, tokens.reshape(piece, width), out_cotangent.reshape(piece, width), segment_ids, valid_mask,
        *parts, qv_bias, *vectors
    )
    if raw:
        lo, tg, g_qkv, g_qv, g_out, g_in, g_down, *sums, rms = run_finish(cols, *results)
        return (
            lo.reshape(1, piece, width), tg.reshape(1, piece, width), g_qkv, g_qv, g_out, sums[0], sums[1], sums[2],
            g_in, sums[3], g_down.T, sums[4], sums[5], sums[6], rms.reshape(-1),
        )
    lo, tg, ga, gi, gd, small = results
    ga, gi, gd = (lax.psum_scatter(g, "ctx", scatter_dimension=0, tiled=True) for g in (ga, gi, gd))
    g_qkv = jnp.stack([ga[:, 2 * cols:3 * cols], ga[:, 0:cols], ga[:, cols:2 * cols]])
    sums = jnp.sum(small[6:9], axis=1)
    return (
        lo.reshape(1, piece, width),
        tg.reshape(1, piece, width).astype(F32),
        g_qkv,
        jnp.stack([small[18, 0:cols], small[17, cols:2 * cols]]),
        ga[:, 3 * cols:].T,
        small[0], small[1], small[2],
        gi,
        small[16],
        gd.T,
        small[3], small[4], small[5],
        jnp.sqrt(sums / (small[9, 0] * width)),
    )


def solution(mesh):
    sizes = (mesh.shape["shard"], mesh.shape["ctx"])
    return jax.shard_map(
        functools.partial(body, sizes),
        mesh=mesh,
        in_specs=(
            P("shard", "ctx", None), P("shard", "ctx"), P("shard", "ctx"),
            P(None, ("shard", "ctx"), "tp"), P(None, "tp"), P("tp", ("shard", "ctx")),
            P(), P(), P(),
            P(("shard", "ctx"), "tp"), P("tp"), P("tp", ("shard", "ctx")),
            P(), P(), P(),
            P("shard", "ctx", None),
        ),
        out_specs=(
            P("shard", "ctx", None), P("shard", "ctx", None),
            P(None, ("shard", "ctx"), "tp"), P(None, "tp"), P("tp", ("shard", "ctx")),
            P(), P(), P(),
            P(("shard", "ctx"), "tp"), P("tp"), P("tp", ("shard", "ctx")),
            P(), P(), P(), P(),
        ),
        check_vma=False,
    )
```

time: 165 us -> 149 us (0.903)
  Pallas kernels: 163 us -> 147 us
    pallas_call x1, Pallas kernels: 159 us -> 144 us  [run_layer(): pl.pallas_call(functools.partial(layer_kernel, dims), out_shape=(jax.Shap...]
where the time goes in v3:
time: 149 us; the launch traced here: 148 us
  Pallas kernels  147 us (99%)
    pallas_call x1, Pallas kernels, run_layer(): pl.pallas_call(functools.partial(layer_kernel, dims), out_shape=(jax.Shap...  144 us
    pallas_call x1, Pallas kernels, run_finish(): pl.pallas_call(functools.partial(finish_kernel, cols), out_shape=tuple((j...  3.68 us

profile of v3, /device:TPU:0, one launch (start us, length us, event | category | flops | bytes accessed | tf_op | source)
XLA Modules:
  0.0 148.2 jit_solution(13340699736870430828)
XLA Ops:
  0.7 143.7 %layer.1 = (bf16[4,128,768]{2,1,0:T(8,128)(2,1)}, bf16[4,128,768]{2,1,0:T(8,128)(2,1)}, f32[96,768]{1,0:T(8,128)}, f32[96,768]{1,0:T(8,128)}, f32[96,768]{1,0:T(8,128)}, /*index=5*/f32[24,768]{1,0:T(8,128)}) custom-call(bf16[512,768]{1,0:T(8,128)(2,1)} %bitcast.8, f32[512,768]{1,0:T(8,128)} %bitcast.7, s32[1,512]{1,0:T(1,128)} %refs_2_.1, s32[1,512]{1,0:T(1,128)} %refs_3_.1, ...), custom_call_target="tpu_custom_call" | custom-call | tf_op jit(solution)/shard_map/layer/pallas_call | solution.py:571
  144.3 3.7 %finish.1 = (bf16[4,128,768]{2,1,0:T(8,128)(2,1)}, f32[4,128,768]{2,1,0:T(8,128)}, f32[3,96,192]{2,1,0:T(8,128)}, f32[2,192]{1,0:T(2,128)}, f32[192,96]{1,0:T(8,...) custom-call(bf16[4,128,768]{2,1,0:T(8,128)(2,1)} %get-tuple-element., ...), custom_call_target="tpu_custom_call" | custom-call | tf_op jit(solution)/shard_map/finish/pallas_call | solution.py:621

commit v4 on v3

v4 whole, which is shorter than its diff:
```python
import functools

import jax
import jax.numpy as jnp
from jax import lax
from jax.experimental import pallas as pl
from jax.experimental.pallas import tpu as pltpu
from jax.sharding import PartitionSpec as P

HEAD_DIM = 64
LANES = 128
TP = 4
EPS = 1e-12
MASKED = -1e30
F32 = jnp.float32
BF16 = jnp.bfloat16
BLOCKS = 4
COPIES = 320
IN_RANGES = ((0, 768, False),)
DOWN_RANGES = ((0, 384, True), (384, 768, False))
IN_SUMS = ((0, 768, False),)
DOWN_SUMS = ((0, 384, True), (384, 768, False))
QO_TURN = False
ORDER = (
    "A0A1B0A2B1A3X5B2B3X2X6C0D0C1D1C2D2P0C3P1E0D3P2E1P3",
    "E2F0E3G0F1H0F2G1G2H1I0F3H2G3X0I1H3X3I2I3X4X1",
)


def nt(left, right):
    return lax.dot_general(left, right, (((1,), (1,)), ((), ())), preferred_element_type=F32)


def nn(left, right):
    return lax.dot_general(left, right, (((1,), (0,)), ((), ())), preferred_element_type=F32)


def gelu_and_slope(pre):
    scale = 0.7978845608028654
    cube = 0.044715
    square = pre * pre
    tanh = jnp.tanh(scale * pre * (1.0 + cube * square))
    half = 0.5 * (1.0 + tanh)
    slope = half + 0.5 * pre * (1.0 - tanh * tanh) * (scale * (1.0 + 3.0 * cube * square))
    return pre * half, slope


def column_sum(rows):
    return jnp.sum(rows, axis=0, keepdims=True)


def norm_forward(rows):
    mean = jnp.mean(rows, axis=-1, keepdims=True)
    centred = rows - mean
    spread = jnp.mean(centred * centred, axis=-1, keepdims=True)
    inverse = lax.rsqrt(spread + EPS)
    return centred * inverse, inverse


def norm_backward(grad, unit, inverse, gain):
    scaled = grad * gain
    first = jnp.mean(scaled, axis=-1, keepdims=True)
    second = jnp.mean(scaled * unit, axis=-1, keepdims=True)
    return inverse * (scaled - first - unit * second)


class Net:
    def __init__(self, send_sems, recv_sems):
        self.send_sems, self.recv_sems, self.copies = send_sems, recv_sems, []

    def send(self, source, target, where, when=None, place=None):
        number = len(self.copies)
        copy = pltpu.make_async_remote_copy(
            src_ref=source,
            dst_ref=target,
            send_sem=self.send_sems.at[number],
            recv_sem=self.recv_sems.at[number if place is None else place],
            device_id=where,
            device_id_type=pl.DeviceIdType.MESH,
        )
        self.copies.append((copy, when))
        if when is None:
            copy.start()
        else:
            pl.when(when)(copy.start)
        copy.number = number
        return copy

    def finish(self):
        for copy, when in self.copies:
            if when is None:
                copy.wait_send()
            else:
                pl.when(when)(copy.wait_send)


def layer_kernel(dims, *refs):
    shards, ctxs, wctx, piece, width, chunk, heads = dims
    rows_b = piece // BLOCKS
    half = rows_b // 2
    cols = heads * HEAD_DIM
    (x_ref, cot_ref, qkv_ref, out_ref, wi_ref, wd_ref, seg_ref, valid_ref, qv_bias_ref, out_bias_ref, gain1_ref,
     shift1_ref, in_bias_ref, down_bias_ref, gain2_ref, shift2_ref,
     lo_ref, tg_ref, ga_ref, gi_ref, gd_ref, small_ref,
     wa, wi, wd, xt, yt, xs, code_all, bias, kv, kvt, qm, sbuf, pt, pt_r, ott, mt, vcol, cot,
     hid, act, slope, dffn, dpre, datt, datt_r, lobuf, tgbuf,
     part, near_in, far_out, far_in, gown, gxs, gxr, gzs, gzr, dkv0, dqt, dproj, dqp, ctxp, dom0, dom1,
     unit1, hidden, resid, sa, sb,
     sa1, sac, sas, sbc, sbs,
     qkv_own, out_own, code_ref, vec_ref, stat, stat_in, delta, delta_in,
     local_sems, send_sems, recv_sems) = refs
    me_s, me_c, me_t = lax.axis_index("shard"), lax.axis_index("ctx"), lax.axis_index("tp")
    mine = me_t % 2
    other = 1 - mine
    near = {"tp": me_t + 1 - 2 * mine}
    far = {"tp": (me_t + 2) % TP}
    wc = me_c if wctx > 1 else 0
    net = Net(send_sems, recv_sems)

    def shard_at(step):
        return (me_s + step) % shards

    def ctx_at(step):
        return (me_c + step) % ctxs

    line = shards == 4
    steps = [2, 1, 3] if line else list(range(1, shards))
    side = me_s // 2
    is_hub = (me_s + side) % 2 == 1
    partner, other_hub, other_end = me_s + 1 - 2 * (me_s % 2), 2 - side, 3 - 3 * side

    barrier = pltpu.get_barrier_semaphore()
    local = {}

    def fetch(name, source, target):
        local[name] = pltpu.make_async_copy(source, target, local_sems.at[len(local)])
        local[name].start()

    own_a, own_i, own_d = wa.at[me_s, wc], wi.at[me_s, wc], wd.at[me_s, wc]
    if wctx < ctxs:
        fetch("qkv", qkv_ref, own_a)
    else:
        fetch("qkv", qkv_ref, qkv_own)
        fetch("out", out_ref, out_own)
    fetch("x", x_ref, xs.at[0])
    fetch("wi", wi_ref, own_i)
    fetch("wd", wd_ref, own_d)
    peers = [near, far]
    peers += [{"ctx": ctx_at(e)} for e in range(1, ctxs)]
    peers += [{"shard": shard_at(d)} for d in range(1, shards)]
    for peer in peers:
        pl.semaphore_signal(barrier, inc=1, device_id=peer, device_id_type=pl.DeviceIdType.MESH)
    local["qkv"].wait()
    if wctx == ctxs:
        local["out"].wait()
        wa[me_s, wc, :, 0:cols] = qkv_own[1]
        wa[me_s, wc, :, cols:2 * cols] = qkv_own[2]
        wa[me_s, wc, :, 2 * cols:3 * cols] = qkv_own[0]
        wa[me_s, wc, :, 3 * cols:] = jnp.transpose(out_own[...].astype(F32)).astype(BF16)
    local["x"].wait()
    pl.semaphore_wait(barrier, len(peers))

    class Gather:
        def __init__(self, buf, lo, hi, turn=False):
            self.buf, self.span, self.turn = buf, slice(lo, hi), turn and wctx > 1
            self.along, self.across = {}, []

        def piece(self, s, c):
            return self.buf.at[s, c, :, self.span]

        def send_along(self, c):
            reach = {1: me_s != 3, 3: me_s != 0} if line else {}
            own = self.piece(me_s, {"own": wc, "peer": 1 - wc}.get(c, 0))
            for d in steps:
                self.along[c, d] = net.send(own, own, {"shard": shard_at(d)}, reach.get(d))

        def send_across(self, s):
            if wctx > 1:
                piece = self.piece(s, wc)
                self.across.append(net.send(piece, piece, {"ctx": ctx_at(1)}))

        def start(self):
            self.send_along(0 if wctx == 1 else "own")

        def start_across(self):
            self.send_across(me_s)

        def second(self):
            if self.turn:
                self.across[0].wait_recv()
                self.send_along("peer")

        def arrive(self, name, d):
            c = {"own": wc, "peer": 1 - wc}.get(name, 0)
            self.along[name, d].wait_recv()
            s = shard_at(shards - d)
            if line and d == 2:
                piece = self.piece(s, c)
                net.send(piece, piece, {"shard": 3}, me_s == 2, self.along[name, 3].number)
                net.send(piece, piece, {"shard": 0}, me_s == 1, self.along[name, 1].number)
            if name == "own" and not self.turn:
                self.send_across(s)

        def middle(self):
            if line:
                for name, d in list(self.along):
                    if d == 2:
                        self.arrive(name, d)

        def rest(self):
            for name, d in list(self.along):
                if d != 2 or not line:
                    self.arrive(name, d)

        def wait(self):
            for copy in self.across[1 if self.turn else 0:]:
                copy.wait_recv()

    def wait_all(copies):
        for copy in copies:
            copy.wait_recv()

    def whole(buf, lo, hi):
        return buf[:, :, :, lo:hi].reshape(width, hi - lo)

    def sum_start(k, b, value):
        part[k, b] = value.reshape(2, half, width)
        return net.send(part.at[k, b, other], near_in.at[k, b], near)

    def sum_pass(k, b, copy):
        copy.wait_recv()
        far_out[k, b] = (part[k, b, mine] + near_in[k, b]).astype(BF16)
        return net.send(far_out.at[k, b], far_in.at[k, b], far)

    def sum_end(k, b, copy):
        copy.wait_recv()
        return far_out[k, b].astype(F32) + far_in[k, b].astype(F32)

    def share(buf, b, value):
        buf[b, mine] = value
        return net.send(buf.at[b, mine], buf.at[b, mine], near)

    def block(b):
        return slice(b * rows_b, (b + 1) * rows_b)

    def own_rows(b):
        return pl.ds(pl.multiple_of(b * rows_b + mine * half, half), half)

    roles = [other_end, other_hub, partner, me_s] if line else [shard_at(d) for d in range(1, shards)] + [me_s]

    class Sums:
        def __init__(self, k, lo, hi, turn=False):
            self.k, self.span, self.turn = k, slice(lo, hi), turn and wctx > 1
            self.across, self.copies = {}, {}

        def term(self, s, c):
            if c:
                return gxs[self.k, s, :, self.span].astype(F32)
            total = gown[self.k, s, :, self.span]
            if wctx > 1 and not self.turn:
                total = total + gxr[self.k, s, :, self.span].astype(F32)
            return total

        def out_slot(self, c, r):
            return gzs.at[c, self.k, r, :, self.span]

        def in_slot(self, c, r):
            return gzr.at[c, self.k, r, :, self.span]

        def passes(self):
            return (1, 0) if self.turn else (0,)

        def start(self, which=None):
            if wctx == 1 or self.turn:
                return
            for r in range(shards) if which is None else which:
                s = roles[r]
                self.across[r] = net.send(
                    gxs.at[self.k, s, :, self.span], gxr.at[self.k, s, :, self.span], {"ctx": ctx_at(1)}
                )

        def along(self):
            outer = jnp.logical_not(is_hub)
            for r in range(shards - 1):
                if r in self.across:
                    self.across[r].wait_recv()
                for c in self.passes():
                    if line and r < 2:

                        @pl.when(outer)
                        def _():
                            gzs[c, self.k, r, :, self.span] = self.term(roles[r], c).astype(BF16)

                        self.copies[c, r] = net.send(
                            self.out_slot(c, r), self.in_slot(c, r), {"shard": partner}, outer
                        )
                    else:
                        gzs[c, self.k, r, :, self.span] = self.term(roles[r], c).astype(BF16)
                        self.copies[c, r] = net.send(
                            self.out_slot(c, r), self.in_slot(c, r), {"shard": roles[r]}
                        )

        def merge(self):
            if not line:
                return
            for r in range(2):
                for c in self.passes():

                    @pl.when(is_hub)
                    def _():
                        self.copies[c, r].wait_recv()
                        total = self.term(roles[r], c) + gzr[c, self.k, r, :, self.span].astype(F32)
                        gzs[c, self.k, r, :, self.span] = total.astype(BF16)

                    place = self.copies[c, 3].number if r else None
                    copy = net.send(self.out_slot(c, r), self.in_slot(c, 3), {"shard": roles[r]}, is_hub, place)
                    if r == 0:
                        self.copies[c, 3] = copy

        def total(self, c):
            value = self.term(me_s, c)
            for r in (2, 3) if line else range(shards - 1):
                self.copies[c, r].wait_recv()
                value = value + gzr[c, self.k, r, :, self.span].astype(F32)
            return value

        def turned(self):
            if not self.turn:
                return
            gzs[1, self.k, 3, :, self.span] = self.total(1).astype(BF16)
            self.final = net.send(self.out_slot(1, 3), gxr.at[self.k, me_s, :, self.span], {"ctx": ctx_at(1)})

        def end(self, out_ref):
            if shards - 1 in self.across:
                self.across[shards - 1].wait_recv()
            value = self.total(0)
            if self.turn:
                self.final.wait_recv()
                value = value + gxr[self.k, me_s, :, self.span].astype(F32)
            out_ref[:, self.span] = value

    g_down = [Sums(2, *r) for r in DOWN_SUMS]
    g_in = [Sums(1, *r) for r in IN_SUMS]
    g_kv, g_qo = Sums(0, 0, 2 * cols), Sums(0, 2 * cols, width, QO_TURN)

    def each(items, name, *args):
        for item in items:
            getattr(item, name)(*args)

    def grad_product(k, lo, terms):
        for c in range(wctx - 1, -1, -1):
            where = (me_c + c) % wctx if wctx > 1 else 0
            value = 0.0
            for left, right in terms:
                value = value + nn(left[where].reshape(shards * chunk, piece), right)
            n = value.shape[1]
            value = value.reshape(shards, chunk, n)
            if c > 0:
                gxs[k, :, :, lo:lo + n] = value.astype(BF16)
            else:
                gown[k, :, :, lo:lo + n] = value

    def store_transposed(target, value):
        turned = jnp.transpose(value)
        for s in range(shards):
            for c in range(wctx):
                begin = (s * wctx + c) * chunk
                target[c, s] = turned[begin:begin + chunk]

    def exchange(buf, source, axis, at, count, me):
        buf[me] = source
        return [net.send(buf.at[me], buf.at[me], {axis: at(e)}) for e in range(1, count)]

    def exchange_end(buf, state, count):
        wait_all(state)
        total = buf[0]
        for i in range(1, count):
            total = total + buf[i]
        return total

    quarter = piece // TP

    def token_rows(t):
        return pl.ds(pl.multiple_of(t * quarter, quarter), quarter)

    me_rows, far_rows = token_rows(me_t), token_rows((me_t + 2) % TP)
    split = 2 * cols
    w_kv, w_qo = Gather(wa, 0, split), Gather(wa, split, width, True)
    w_in = [Gather(wi, *r) for r in IN_RANGES]
    w_down = [Gather(wd, *r) for r in DOWN_RANGES]
    w_kv.start()
    w_qo.start_across()
    token_in = [
        net.send(xs.at[0, me_rows], xs.at[e, me_rows], {"ctx": ctx_at(e)}) for e in range(1, ctxs)
    ]
    w_kv.start_across()
    w_qo.start()
    seg = seg_ref[...].astype(F32)
    real = valid_ref[...] == 1
    code_ref[...] = jnp.zeros_like(code_ref)
    code_ref[0:1] = jnp.where(real, seg, -1.0)
    code_ref[1:2] = seg
    code_ref[2:3] = jnp.where(real, 1.0, 0.0)
    code_sends = [net.send(code_ref, code_all.at[e], {"ctx": ctx_at(e)}) for e in range(1, ctxs)]
    code_all[0] = code_ref[...]
    for b in range(BLOCKS):
        fetch("cot%d" % b, cot_ref.at[own_rows(b)], cot.at[b])
    vec_ref[...] = jnp.zeros_like(vec_ref)
    vec_ref[0:1, 0:cols] = qv_bias_ref[0:1]
    vec_ref[1:2, cols:2 * cols] = qv_bias_ref[1:2]
    vcol[...] = jnp.transpose(jnp.broadcast_to(code_ref[2:3, :], (LANES, piece)))
    w_qo.second()
    w_kv.middle()
    token_far, token_near = [], []
    for e in range(1, ctxs):
        token_in[e - 1].wait_recv()
        token_far.append(net.send(xs.at[e, me_rows], xs.at[e, me_rows], far))
        token_near.append(net.send(xs.at[e, me_rows], xs.at[e, me_rows], near))

    def column_code(e):
        return jnp.transpose(jnp.broadcast_to(code_all[e][0:1, :], (LANES, piece)))[:, 0:1]

    def store_bias(e):
        allowed = column_code(e) == code_ref[1:2, :]
        if e == 0:
            rows = lax.broadcasted_iota(jnp.int32, (piece, piece), 0)
            lanes = lax.broadcasted_iota(jnp.int32, (piece, piece), 1)
            allowed = allowed | (rows == lanes)
        bias[e] = jnp.where(allowed, 0.0, MASKED)

    store_bias(0)
    w_kv.rest()
    w_qo.middle()
    local["wi"].wait()
    local["wd"].wait()
    for gather in w_in:
        gather.start()
    for e in range(1, ctxs):
        token_far[e - 1].wait_recv()
        token_near.append(net.send(xs.at[e, far_rows], xs.at[e, far_rows], near))
    for gather in w_in + w_down:
        gather.start_across()
    wait_all(code_sends)
    for e in range(1, ctxs):
        store_bias(e)
    w_kv.wait()

    x = xs[0]

    def project_kv(e):
        kv[e] = (nn(xs[e], whole(wa, 0, split)) + vec_ref[1:2, 0:split]).astype(BF16)
        kvt[e] = jnp.transpose(kv[e])

    lane = lax.broadcasted_iota(jnp.int32, (piece, 256), 1)

    def project_q(e):
        low = (nn(xs[e], whole(wa, split, split + 256)) + vec_ref[0:1, 0:256]).astype(BF16).astype(F32) * 0.125
        for h in range(heads):
            inside = (lane >= h * HEAD_DIM) & (lane < (h + 1) * HEAD_DIM)
            qm[e, h] = jnp.where(inside, low, 0.0).astype(BF16)

    project_kv(0)
    w_qo.rest()
    for gather in w_down:
        gather.start()
    w_qo.wait()
    project_q(0)
    wait_all(token_near)
    for e in range(1, ctxs):
        project_kv(e)
    for gather in w_in:
        gather.middle()

    ott[0:cols] = jnp.zeros((cols, piece), F32)
    mt[0:cols] = jnp.zeros((cols, piece), F32)
    stat[...] = jnp.zeros_like(stat)
    delta[...] = jnp.zeros_like(delta)
    for h in range(heads):
        top = None
        for e in range(ctxs):
            s = nt(kv[e][:, 0:256], qm[0, h]) + bias[e]
            sbuf[e] = s
            high = jnp.max(s, axis=0, keepdims=True)
            top = high if top is None else jnp.maximum(top, high)
        rows = slice(cols + h * HEAD_DIM, cols + (h + 1) * HEAD_DIM)
        total = jnp.zeros((1, piece), F32)
        mixed = jnp.zeros((HEAD_DIM, piece), F32)
        for e in range(ctxs):
            weights = jnp.exp(sbuf[e] - top)
            total = total + column_sum(weights)
            low = weights.astype(BF16)
            pt[h, e] = low
            mixed = mixed + nn(kvt[e, rows], low)
        inverse = 1.0 / total
        ott[rows] = mixed * inverse
        mt[rows] = jnp.broadcast_to(inverse, (HEAD_DIM, piece))
        stat[h:h + 1] = top
        stat[4 + h:5 + h] = inverse
        if h == 0:
            for gather in w_in:
                gather.second()
        if h == 1:
            for gather in w_down:
                gather.second()
    stat_sends = [net.send(stat, stat_in.at[e - 1], {"ctx": ctx_at(e)}) for e in range(1, ctxs)]
    ctxp[...] = jnp.transpose(ott[...]).astype(BF16)
    for gather in w_in:
        gather.rest()

    out_bias, gain1, shift1, in_bias = (
        ref[...].reshape(1, -1) for ref in (out_bias_ref, gain1_ref, shift1_ref, in_bias_ref)
    )
    down_bias, gain2, shift2 = (ref[...].reshape(1, -1) for ref in (down_bias_ref, gain2_ref, shift2_ref))
    sa[...] = jnp.zeros_like(sa)
    near_copy, far_copy, share_copy, inverse1, out_copy = {}, {}, {}, {}, {}

    def add_sum(row, value):
        sa[row:row + 1] = sa[row:row + 1] + column_sum(value)

    def stage_a(b):
        near_copy[0, b] = sum_start(0, b, nt(ctxp[block(b)], whole(wa, split, width)))

    def stage_b(b):
        far_copy[0, b] = sum_pass(0, b, near_copy[0, b])

    def stage_c(b):
        attn = sum_end(0, b, far_copy[0, b]) + out_bias
        x_own = xs[0, own_rows(b)].astype(F32)
        valid = vcol[own_rows(b), 0:1]
        unit, inverse1[b] = norm_forward(x_own + attn)
        unit1[b] = unit
        own_hidden = unit * gain1 + shift1
        hidden[b] = own_hidden
        share_copy[0, b] = share(hid, b, own_hidden.astype(BF16))
        add_sum(6, valid * x_own * x_own)
        add_sum(7, valid * attn * attn)
        sa[9:10] = sa[9:10] + column_sum(valid)

    def stage_d(b):
        if b == 0:
            for gather in w_in:
                gather.wait()
        share_copy[0, b].wait_recv()
        pre = nn(hid[b].reshape(rows_b, width), whole(wi, 0, width)) + in_bias
        value, slope[b] = gelu_and_slope(pre)
        act[b] = value.astype(BF16)

    def stage_p(b):
        if b == 0:
            for gather in w_down:
                gather.wait()
        near_copy[1, b] = sum_start(1, b, nt(act[b], whole(wd, 0, width)))

    def stage_e(b):
        far_copy[1, b] = sum_pass(1, b, near_copy[1, b])

    def stage_f(b):
        local["cot%d" % b].wait()
        ffn = sum_end(1, b, far_copy[1, b]) + down_bias
        valid = vcol[own_rows(b), 0:1]
        unit, inverse = norm_forward(hidden[b] + ffn)
        grad = cot[b]
        d_resid2 = norm_backward(grad, unit, inverse, gain2)
        low = d_resid2.astype(BF16)
        share_copy[1, b] = share(dffn, b, low)
        resid[b] = d_resid2
        out_copy[b] = share(lobuf, b, (unit * gain2 + shift2).astype(BF16))
        add_sum(8, valid * ffn * ffn)
        add_sum(3, low.astype(F32))
        add_sum(4, grad * unit)
        add_sum(5, grad)

    def stage_g(b):
        share_copy[1, b].wait_recv()
        d_act = nn(dffn[b].reshape(rows_b, width), whole(wd, 0, width))
        dpre[b] = (d_act * slope[b]).astype(BF16)
        near_copy[2, b] = sum_start(2, b, nt(dpre[b], whole(wi, 0, width)))

    def stage_h(b):
        far_copy[2, b] = sum_pass(2, b, near_copy[2, b])

    def stage_i(b):
        d_hidden = resid[b] + sum_end(2, b, far_copy[2, b])
        unit = unit1[b]
        d_resid1 = norm_backward(d_hidden, unit, inverse1[b], gain1)
        low = d_resid1.astype(BF16)
        share_copy[2, b] = share(datt, b, low)
        resid[b] = d_resid1
        add_sum(0, low.astype(F32))
        add_sum(1, d_hidden * unit)
        add_sum(2, d_hidden)

    stages = dict(A=stage_a, B=stage_b, C=stage_c, D=stage_d, E=stage_e, P=stage_p, F=stage_f, G=stage_g, H=stage_h, I=stage_i)

    def down_grads():
        store_transposed(yt, dffn[...].reshape(piece, width))
        grad_product(2, 0, [(yt, act[...].reshape(piece, width))])
        each(g_down, "start", (0, 1))
        for item in g_down:
            if item.turn:
                item.along()

    def in_grads():
        each(g_down, "start", range(2, shards))
        store_transposed(yt, hid[...].reshape(piece, width))
        grad_product(1, 0, [(yt, dpre[...].reshape(piece, width))])
        each(g_in, "start")
        for item in g_in:
            if item.turn:
                item.along()

    def remote_probs():
        store_transposed(xt, x)
        for e in range(1, ctxs):
            project_q(e)
            bias[e] = jnp.where(column_code(0) == code_all[e][1:2, :], 0.0, MASKED)
            stat_sends[e - 1].wait_recv()
            for h in range(heads):
                s = nt(kv[0][:, 0:256], qm[e, h]) + bias[e]
                pt_r[h, e - 1] = jnp.exp(s - stat_in[e - 1, h:h + 1]).astype(BF16)

    cross = {}

    def cross_send(j):
        b = 2 * j + me_t // 2
        for e in range(1, ctxs):
            cross[j, e] = net.send(datt.at[b, mine], datt_r.at[e - 1, b, mine], {"ctx": ctx_at(e)})

    def cross_pass(j):
        b = 2 * j + me_t // 2
        for e in range(1, ctxs):
            cross[j, e].wait_recv()
            source = datt_r.at[e - 1, b, mine]
            cross[j, e, "far"] = net.send(source, source, far)
            cross[j, e, "near"] = net.send(source, source, near)

    def cross_last(j):
        b = 2 * j + (me_t // 2 + 1) % 2
        for e in range(1, ctxs):
            cross[j, e, "far"].wait_recv()
            source = datt_r.at[e - 1, b, mine]
            cross[j, e, "last"] = net.send(source, source, near)

    def down_middle():
        for gather in w_down:
            gather.middle()

    def down_rest():
        for gather in w_down:
            gather.rest()

    extras = (down_grads, in_grads, remote_probs, lambda: cross_send(0), lambda: cross_send(1), down_middle, down_rest)
    for name in ORDER:
        for i in range(0, len(name), 2):
            if name[i] == "X":
                extras[int(name[i + 1])]()
            else:
                stages[name[i]](int(name[i + 1]))

    sb[...] = jnp.zeros_like(sb)
    sb[0:1] = column_sum(dpre[...].reshape(piece, width).astype(F32))
    sa_near = net.send(sa, sa1, near)
    for b in range(BLOCKS):
        share_copy[2, b].wait_recv()
    lane = lax.broadcasted_iota(jnp.int32, (piece, LANES), 1)

    def mixed_gradient(e, d_att, scale):
        d_mix = nn(d_att, whole(wa, split, width)).astype(BF16).astype(F32) * jnp.transpose(scale)
        dom0[e] = d_mix[:, 0:256].astype(BF16)
        last = d_mix[:, 256:384]
        dom1[e, 0] = jnp.where(lane < HEAD_DIM, last, 0.0).astype(BF16)
        dom1[e, 1] = jnp.where(lane >= HEAD_DIM, last, 0.0).astype(BF16)
        return d_mix

    d_att_all = datt[...].reshape(piece, width)
    d_mix = mixed_gradient(0, d_att_all, mt[...])
    product = jnp.transpose(d_mix)[cols:] * ott[cols:]
    for h in range(heads):
        delta[h:h + 1] = column_sum(product[h * HEAD_DIM:(h + 1) * HEAD_DIM])
    for item in g_down:
        if item.turn:
            item.merge()
        else:
            item.along()
    delta_sends = [net.send(delta, delta_in.at[e - 1], {"ctx": ctx_at(e)}) for e in range(1, ctxs)]
    cross_pass(0)

    def score_gradient(h, keys, queries, probs, deltas):
        if h == 0:
            d_probs = nt(kv[keys][:, 0:256], dom0[queries])
        else:
            d_probs = nt(kv[keys][:, 256:384], dom1[queries, h - 1])
        return (probs.astype(F32) * (d_probs - deltas)).astype(BF16)

    def key_gradient(h, queries, probs, d_scores):
        first = nn(d_scores, qm[queries, h])
        if h == 0:
            dkv0[:, 0:256] = dkv0[:, 0:256] + first + nn(probs, dom0[queries])
        else:
            dkv0[:, 0:256] = dkv0[:, 0:256] + first
            dkv0[:, 256:384] = dkv0[:, 256:384] + nn(probs, dom1[queries, h - 1])

    dkv0[...] = jnp.zeros_like(dkv0)
    dqt[...] = jnp.zeros((2 * cols, piece), F32)
    for e in range(ctxs):
        for h in range(heads):
            d_scores = score_gradient(h, e, 0, pt[h, e], delta[h:h + 1])
            rows = slice(h * HEAD_DIM, (h + 1) * HEAD_DIM)
            dqt[rows] = dqt[rows] + nn(kvt[e, rows], d_scores)
            if e == 0:
                key_gradient(h, 0, pt[h, 0], d_scores)
        if e == 0:
            cross_pass(1)
            cross_last(0)
            for item in g_down:
                if item.turn:
                    item.turned()
                else:
                    item.merge()
    sa_near.wait_recv()
    sa_c = exchange(sac, sa[...] + sa1[...], "ctx", ctx_at, ctxs, me_c)
    cross_last(1)
    dqp[...] = jnp.transpose(dqt[...] * 0.125).astype(BF16)
    store_transposed(yt, d_att_all)
    grad_product(0, split, [(xt, dqp[...]), (yt, ctxp[...])])
    g_qo.start()
    if g_qo.turn:
        g_qo.along()
    sa_s = exchange(sas, exchange_end(sac, sa_c, ctxs), "shard", shard_at, shards, me_s)
    for e in range(1, ctxs):
        for j in range(BLOCKS // 2):
            cross[j, e, "near"].wait_recv()
            cross[j, e, "last"].wait_recv()
        delta_sends[e - 1].wait_recv()
        for h in range(heads):
            rows = slice(cols + h * HEAD_DIM, cols + (h + 1) * HEAD_DIM)
            mt[rows] = jnp.broadcast_to(stat_in[e - 1, 4 + h:5 + h], (HEAD_DIM, piece))
        mixed_gradient(e, datt_r[e - 1].reshape(piece, width), mt[...])
        for h in range(heads):
            probs = pt_r[h, e - 1]
            d_scores = score_gradient(h, 0, e, probs, delta_in[e - 1, h:h + 1])
            key_gradient(h, e, probs, d_scores)
    for item in g_in:
        if item.turn:
            item.merge()
        else:
            item.along()
    dproj[...] = dkv0[...].astype(BF16)

    def back_tokens(b):
        value = nt(dproj[block(b)], whole(wa, 0, split))
        return value + nt(dqp[block(b), 0:256], whole(wa, split, split + 256))

    for b in range(2):
        near_copy[3, b] = sum_start(3, b, back_tokens(b))
    far_copy[3, 0] = sum_pass(3, 0, near_copy[3, 0])
    grad_product(0, 0, [(xt, dproj[...])])
    g_kv.start()
    far_copy[3, 1] = sum_pass(3, 1, near_copy[3, 1])
    for b in range(2, BLOCKS):
        near_copy[3, b] = sum_start(3, b, back_tokens(b))
    for b in range(2, BLOCKS):
        far_copy[3, b] = sum_pass(3, b, near_copy[3, b])
    sb[1:2, 0:split] = column_sum(dproj[...].astype(F32))
    sb[2:3, 0:split] = column_sum(dqp[...].astype(F32))
    sb_c = exchange(sbc, sb[...], "ctx", ctx_at, ctxs, me_c)
    for item in g_in:
        if item.turn:
            item.turned()
        else:
            item.merge()
    if g_qo.turn:
        g_qo.merge()
    else:
        g_qo.along()
    for b in range(BLOCKS):
        share_copy[3, b] = share(tgbuf, b, (resid[b] + sum_end(3, b, far_copy[3, b])).astype(BF16))
    sb_s = exchange(sbs, exchange_end(sbc, sb_c, ctxs), "shard", shard_at, shards, me_s)
    g_kv.along()
    if g_qo.turn:
        g_qo.turned()
    else:
        g_qo.merge()
    each(g_down, "end", gd_ref)
    for b in range(BLOCKS):
        out_copy[b].wait_recv()
        lo_ref[b] = lobuf[b].reshape(rows_b, width)
    small_ref[0:16] = exchange_end(sas, sa_s, shards)
    g_kv.merge()
    each(g_in, "end", gi_ref)
    for b in range(BLOCKS):
        share_copy[3, b].wait_recv()
        tg_ref[b] = tgbuf[b].reshape(rows_b, width)
    small_ref[16:24] = exchange_end(sbs, sb_s, shards)
    g_qo.end(ga_ref)
    g_kv.end(ga_ref)
    net.finish()


def run_layer(dims, copies, *operands):
    shards, ctxs, wctx, piece, width, chunk, heads = dims
    rows_b = piece // BLOCKS
    half = rows_b // 2
    cols = heads * HEAD_DIM
    hidden_cols = operands[4].shape[1]
    vmem = pl.BlockSpec(memory_space=pltpu.VMEM)
    weights = (shards, wctx, chunk, width)
    turned = (wctx, shards, chunk, piece)
    V = pltpu.VMEM
    shared = (BLOCKS, 2, half, width)
    hidden = (BLOCKS, rows_b, hidden_cols)
    scratch = [
        V(weights, BF16), V(weights, BF16), V(weights, BF16),
        V(turned, BF16), V(turned, BF16),
        V((ctxs, piece, width), BF16),
        V((ctxs, 8, piece), F32), V((ctxs, piece, piece), F32),
        V((ctxs, piece, 2 * cols), BF16), V((ctxs, 2 * cols, piece), BF16), V((ctxs, heads, piece, 256), BF16),
        V((ctxs, piece, piece), F32), V((heads, ctxs, piece, piece), BF16), V((heads, ctxs - 1, piece, piece), BF16),
        V((2 * cols, piece), F32), V((2 * cols, piece), F32), V((piece, LANES), F32), V((BLOCKS, half, width), F32),
        V(shared, BF16), V(hidden, BF16), V(hidden, F32),
        V(shared, BF16), V(hidden, BF16), V(shared, BF16), V((ctxs - 1,) + shared, BF16), V(shared, BF16),
        V(shared, BF16),
        V((4, BLOCKS, 2, half, width), F32), V((4, BLOCKS, half, width), F32),
        V((4, BLOCKS, half, width), BF16), V((4, BLOCKS, half, width), BF16),
        V((3, shards, chunk, width), F32), V((3, shards, chunk, width), BF16), V((3, shards, chunk, width), BF16),
        V((wctx, 3, shards, chunk, width), BF16), V((wctx, 3, shards, chunk, width), BF16),
        V((piece, 2 * cols), F32),
        V((2 * cols, piece), F32), V((piece, 2 * cols), BF16), V((piece, 2 * cols), BF16), V((piece, 2 * cols), BF16),
        V((ctxs, piece, 256), BF16), V((ctxs, 2, piece, LANES), BF16),
        V((BLOCKS, half, width), F32), V((BLOCKS, half, width), F32), V((BLOCKS, half, width), F32),
        V((16, width), F32), V((8, width), F32),
        V((16, width), F32), V((ctxs, 16, width), F32), V((shards, 16, width), F32),
        V((ctxs, 8, width), F32), V((shards, 8, width), F32),
        V((3, chunk, cols), BF16), V((cols, chunk), BF16), V((8, piece), F32), V((8, 2 * cols), F32),
        V((8, piece), F32), V((ctxs - 1, 8, piece), F32), V((8, piece), F32), V((ctxs - 1, 8, piece), F32),
        pltpu.SemaphoreType.DMA((BLOCKS + 5,)), pltpu.SemaphoreType.DMA((copies,)),
        pltpu.SemaphoreType.DMA((copies,)),
    ]
    return pl.pallas_call(
        functools.partial(layer_kernel, dims),
        out_shape=(
            jax.ShapeDtypeStruct((BLOCKS, rows_b, width), BF16),
            jax.ShapeDtypeStruct((BLOCKS, rows_b, width), BF16),
            jax.ShapeDtypeStruct((chunk, width), F32),
            jax.ShapeDtypeStruct((chunk, hidden_cols), F32),
            jax.ShapeDtypeStruct((chunk, hidden_cols), F32),
            jax.ShapeDtypeStruct((24, width), F32),
        ),
        in_specs=[pl.BlockSpec(memory_space=pl.ANY)] * 6 + [vmem] * (len(operands) - 6),
        out_specs=(vmem,) * 6,
        scratch_shapes=scratch,
        compiler_params=pltpu.CompilerParams(
            collective_id=0, has_side_effects=True, vmem_limit_bytes=67_043_328
        ),
        name="layer",
    )(*operands)


def finish_kernel(cols, *refs):
    (lo, tg, ga, gi, gd, small,
     lo_out, tg_out, qkv_out, qv_out, out_out, in_out, down_out, v0, v1, v2, v3, v4, v5, v6, rms_out) = refs
    lo_out[...] = lo[...]
    tg_out[...] = tg[...].astype(F32)
    qkv_out[0] = ga[:, 2 * cols:3 * cols]
    qkv_out[1] = ga[:, 0:cols]
    qkv_out[2] = ga[:, cols:2 * cols]
    out_out[...] = jnp.transpose(ga[:, 3 * cols:])
    in_out[...] = gi[...]
    down_out[...] = gd[...]
    qv_out[0:1] = small[18:19, 0:cols]
    qv_out[1:2] = small[17:18, cols:2 * cols]
    for row, ref in zip((0, 1, 2, 16, 3, 4, 5), (v0, v1, v2, v3, v4, v5, v6)):
        ref[...] = small[row]
    count = small[9:10, 0:1] * small.shape[1]
    for i in range(3):
        rms_out[0:1, i:i + 1] = jnp.sqrt(jnp.sum(small[6 + i:7 + i], axis=1, keepdims=True) / count)


def run_finish(cols, *operands):
    _, rows_b, width = operands[0].shape
    chunk, hidden_cols = operands[3].shape
    shapes = [
        ((BLOCKS, rows_b, width), BF16), ((BLOCKS, rows_b, width), F32), ((3, chunk, cols), F32), ((2, cols), F32),
        ((cols, chunk), F32), ((chunk, hidden_cols), F32), ((chunk, hidden_cols), F32),
        ((width,), F32), ((width,), F32), ((width,), F32), ((hidden_cols,), F32),
        ((width,), F32), ((width,), F32), ((width,), F32), ((1, 3), F32),
    ]
    vmem = pl.BlockSpec(memory_space=pltpu.VMEM)
    return pl.pallas_call(
        functools.partial(finish_kernel, cols),
        out_shape=tuple(jax.ShapeDtypeStruct(*shape) for shape in shapes),
        in_specs=[vmem] * len(operands),
        out_specs=(vmem,) * len(shapes),
        name="finish",
    )(*operands)


def body(
    sizes,
    tokens, segment_ids, valid_mask, qkv_weight, qv_bias, out_weight, out_bias, norm1_gain, norm1_shift,
    in_weight, in_bias, down_weight, down_bias, norm2_gain, norm2_shift, out_cotangent,
):
    shards, ctxs = sizes
    _, piece, width = tokens.shape
    cols = qkv_weight.shape[2]
    heads = cols // HEAD_DIM
    raw = qkv_weight.shape[1] % 16 == 0 and ctxs <= 2
    if raw:
        wctx = ctxs
        parts = [qkv_weight, out_weight, in_weight, down_weight.T]
        chunk = in_weight.shape[0]
    else:
        wctx = 1
        own = jnp.concatenate([qkv_weight[1], qkv_weight[2], qkv_weight[0], out_weight.T], axis=1)
        own, into, down = (
            lax.all_gather(part, "ctx", axis=0, tiled=True) for part in (own, in_weight, down_weight.T)
        )
        parts = [own, out_weight, into, down]
        chunk = own.shape[0]
    dims = (shards, ctxs, wctx, piece, width, chunk, heads)
    vectors = [out_bias, norm1_gain, norm1_shift, in_bias, down_bias, norm2_gain, norm2_shift]
    results = run_layer(
        dims, COPIES, tokens.reshape(piece, width), out_cotangent.reshape(piece, width), *parts,
        segment_ids, valid_mask, qv_bias, *vectors
    )
    if raw:
        lo, tg, g_qkv, g_qv, g_out, g_in, g_down, *sums, rms = run_finish(cols, *results)
        return (
            lo.reshape(1, piece, width), tg.reshape(1, piece, width), g_qkv, g_qv, g_out, sums[0], sums[1], sums[2],
            g_in, sums[3], g_down.T, sums[4], sums[5], sums[6], rms.reshape(-1),
        )
    lo, tg, ga, gi, gd, small = results
    ga, gi, gd = (lax.psum_scatter(g, "ctx", scatter_dimension=0, tiled=True) for g in (ga, gi, gd))
    g_qkv = jnp.stack([ga[:, 2 * cols:3 * cols], ga[:, 0:cols], ga[:, cols:2 * cols]])
    sums = jnp.sum(small[6:9], axis=1)
    return (
        lo.reshape(1, piece, width),
        tg.reshape(1, piece, width).astype(F32),
        g_qkv,
        jnp.stack([small[18, 0:cols], small[17, cols:2 * cols]]),
        ga[:, 3 * cols:].T,
        small[0], small[1], small[2],
        gi,
        small[16],
        gd.T,
        small[3], small[4], small[5],
        jnp.sqrt(sums / (small[9, 0] * width)),
    )


def solution(mesh):
    sizes = (mesh.shape["shard"], mesh.shape["ctx"])
    return jax.shard_map(
        functools.partial(body, sizes),
        mesh=mesh,
        in_specs=(
            P("shard", "ctx", None), P("shard", "ctx"), P("shard", "ctx"),
            P(None, ("shard", "ctx"), "tp"), P(None, "tp"), P("tp", ("shard", "ctx")),
            P(), P(), P(),
            P(("shard", "ctx"), "tp"), P("tp"), P("tp", ("shard", "ctx")),
            P(), P(), P(),
            P("shard", "ctx", None),
        ),
        out_specs=(
            P("shard", "ctx", None), P("shard", "ctx", None),
            P(None, ("shard", "ctx"), "tp"), P(None, "tp"), P("tp", ("shard", "ctx")),
            P(), P(), P(),
            P(("shard", "ctx"), "tp"), P("tp"), P("tp", ("shard", "ctx")),
            P(), P(), P(), P(),
        ),
        check_vma=False,
    )
```

time: 149 us -> 139 us (0.933)
  Pallas kernels: 147 us -> 138 us
    pallas_call x1, Pallas kernels: 144 us -> 135 us  [run_layer(): pl.pallas_call(functools.partial(layer_kernel, dims), out_shape=(jax.Shap...]
where the time goes in v4:
time: 139 us
  Pallas kernels  138 us (99%)
    pallas_call x1, Pallas kernels, run_layer(): pl.pallas_call(functools.partial(layer_kernel, dims), out_shape=(jax.Shap...  135 us
    pallas_call x1, Pallas kernels, run_finish(): pl.pallas_call(functools.partial(finish_kernel, cols), out_shape=tuple((j...  3.68 us

profile of v4, /device:TPU:0, one launch (start us, length us, event | category | flops | bytes accessed | tf_op | source)
XLA Modules:
  0.0 139.1 jit_solution(18162308225666652952)
XLA Ops:
  0.7 134.6 %layer.1 = (bf16[4,128,768]{2,1,0:T(8,128)(2,1)}, bf16[4,128,768]{2,1,0:T(8,128)(2,1)}, f32[96,768]{1,0:T(8,128)}, f32[96,768]{1,0:T(8,128)}, f32[96,768]{1,0:T(8,128)}, /*index=5*/f32[24,768]{1,0:T(8,128)}) custom-call(bf16[512,768]{1,0:T(8,128)(2,1)} %bitcast.8, f32[512,768]{1,0:T(8,128)} %bitcast.7, bf16[3,96,192]{2,1,0:T(8,128)(2,1)} %refs_2_.1, ...), custom_call_target="tpu_custom_call" | custom-call | tf_op jit(solution)/shard_map/layer/pallas_call | solution.py:839
  135.3 3.7 %finish.1 = (bf16[4,128,768]{2,1,0:T(8,128)(2,1)}, f32[4,128,768]{2,1,0:T(8,128)}, f32[3,96,192]{2,1,0:T(8,128)}, f32[2,192]{1,0:T(2,128)}, f32[192,96]{1,0:T(8,...) custom-call(bf16[4,128,768]{2,1,0:T(8,128)(2,1)} %get-tuple-element., ...), custom_call_target="tpu_custom_call" | custom-call | tf_op jit(solution)/shard_map/finish/pallas_call | solution.py:889

commit v5 on v4

--- a/solution.py
+++ b/solution.py
@@ -18,9 +18,10 @@
 COPIES = 320
 IN_RANGES = ((0, 768, False),)
 DOWN_RANGES = ((0, 384, True), (384, 768, False))
-IN_SUMS = ((0, 768, False),)
+IN_SUMS = ((0, 384, True), (384, 768, False))
 DOWN_SUMS = ((0, 384, True), (384, 768, False))
 QO_TURN = False
+QO_FIRST = False
 ORDER = (
     "A0A1B0A2B1A3X5B2B3X2X6C0D0C1D1C2D2P0C3P1E0D3P2E1P3",
     "E2F0E3G0F1H0F2G1G2H1I0F3H2G3X0I1H3X3I2I3X4X1",
@@ -385,7 +386,7 @@
 
     me_rows, far_rows = token_rows(me_t), token_rows((me_t + 2) % TP)
     split = 2 * cols
-    w_kv, w_qo = Gather(wa, 0, split), Gather(wa, split, width, True)
+    w_kv, w_qo = Gather(wa, 0, split), Gather(wa, split, width, QO_FIRST)
     w_in = [Gather(wi, *r) for r in IN_RANGES]
     w_down = [Gather(wd, *r) for r in DOWN_RANGES]
     w_kv.start()
@@ -433,7 +434,7 @@
     w_qo.middle()
     local["wi"].wait()
     local["wd"].wait()
-    for gather in w_in:
+    for gather in w_in + w_down:
         gather.start()
     for e in range(1, ctxs):
         token_far[e - 1].wait_recv()
@@ -461,15 +462,17 @@
 
     project_kv(0)
     w_qo.rest()
-    for gather in w_down:
-        gather.start()
+    for gather in w_in + w_down:
+        gather.second()
+    for gather in w_in:
+        gather.middle()
     w_qo.wait()
     project_q(0)
     wait_all(token_near)
     for e in range(1, ctxs):
         project_kv(e)
     for gather in w_in:
-        gather.middle()
+        gather.rest()
 
     ott[0:cols] = jnp.zeros((cols, piece), F32)
     mt[0:cols] = jnp.zeros((cols, piece), F32)
@@ -496,16 +499,8 @@
         mt[rows] = jnp.broadcast_to(inverse, (HEAD_DIM, piece))
         stat[h:h + 1] = top
         stat[4 + h:5 + h] = inverse
-        if h == 0:
-            for gather in w_in:
-                gather.second()
-        if h == 1:
-            for gather in w_down:
-                gather.second()
     stat_sends = [net.send(stat, stat_in.at[e - 1], {"ctx": ctx_at(e)}) for e in range(1, ctxs)]
     ctxp[...] = jnp.transpose(ott[...]).astype(BF16)
-    for gather in w_in:
-        gather.rest()
 
     out_bias, gain1, shift1, in_bias = (
         ref[...].reshape(1, -1) for ref in (out_bias_ref, gain1_ref, shift1_ref, in_bias_ref)
@@ -677,13 +672,11 @@
     product = jnp.transpose(d_mix)[cols:] * ott[cols:]
     for h in range(heads):
         delta[h:h + 1] = column_sum(product[h * HEAD_DIM:(h + 1) * HEAD_DIM])
+    delta_sends = [net.send(delta, delta_in.at[e - 1], {"ctx": ctx_at(e)}) for e in range(1, ctxs)]
+    cross_pass(0)
     for item in g_down:
         if item.turn:
             item.merge()
-        else:
-            item.along()
-    delta_sends = [net.send(delta, delta_in.at[e - 1], {"ctx": ctx_at(e)}) for e in range(1, ctxs)]
-    cross_pass(0)
 
     def score_gradient(h, keys, queries, probs, deltas):
         if h == 0:
@@ -713,19 +706,24 @@
             cross_pass(1)
             cross_last(0)
             for item in g_down:
-                if item.turn:
-                    item.turned()
-                else:
-                    item.merge()
+                if not item.turn:
+                    item.along()
     sa_near.wait_recv()
     sa_c = exchange(sac, sa[...] + sa1[...], "ctx", ctx_at, ctxs, me_c)
     cross_last(1)
+    each(g_down, "turned")
+    for item in g_in:
+        if item.turn:
+            item.merge()
     dqp[...] = jnp.transpose(dqt[...] * 0.125).astype(BF16)
     store_transposed(yt, d_att_all)
     grad_product(0, split, [(xt, dqp[...]), (yt, ctxp[...])])
     g_qo.start()
     if g_qo.turn:
         g_qo.along()
+    for item in g_down:
+        if not item.turn:
+            item.merge()
     sa_s = exchange(sas, exchange_end(sac, sa_c, ctxs), "shard", shard_at, shards, me_s)
     for e in range(1, ctxs):
         for j in range(BLOCKS // 2):
@@ -742,7 +740,7 @@
             key_gradient(h, e, probs, d_scores)
     for item in g_in:
         if item.turn:
-            item.merge()
+            item.turned()
         else:
             item.along()
     dproj[...] = dkv0[...].astype(BF16)
@@ -765,9 +763,7 @@
     sb[2:3, 0:split] = column_sum(dqp[...].astype(F32))
     sb_c = exchange(sbc, sb[...], "ctx", ctx_at, ctxs, me_c)
     for item in g_in:
-        if item.turn:
-            item.turned()
-        else:
+        if not item.turn:
             item.merge()
     if g_qo.turn:
         g_qo.merge()

time: 139 us -> 128 us (0.921)
  Pallas kernels: 138 us -> 127 us
    pallas_call x1, Pallas kernels: 135 us -> 123 us  [run_layer(): pl.pallas_call(functools.partial(layer_kernel, dims), out_shape=(jax.Shap...]
where the time goes in v5:
time: 128 us; the launch traced here: 127 us
  Pallas kernels  127 us (99%)
    pallas_call x1, Pallas kernels, run_layer(): pl.pallas_call(functools.partial(layer_kernel, dims), out_shape=(jax.Shap...  123 us
    pallas_call x1, Pallas kernels, run_finish(): pl.pallas_call(functools.partial(finish_kernel, cols), out_shape=tuple((j...  3.68 us

profile of v5, /device:TPU:0, one launch (start us, length us, event | category | flops | bytes accessed | tf_op | source)
XLA Modules:
  0.0 127.5 jit_solution(4501091969062623252)
XLA Ops:
  0.7 122.9 %layer.1 = (bf16[4,128,768]{2,1,0:T(8,128)(2,1)}, bf16[4,128,768]{2,1,0:T(8,128)(2,1)}, f32[96,768]{1,0:T(8,128)}, f32[96,768]{1,0:T(8,128)}, f32[96,768]{1,0:T(8,128)}, /*index=5*/f32[24,768]{1,0:T(8,128)}) custom-call(bf16[512,768]{1,0:T(8,128)(2,1)} %bitcast.8, f32[512,768]{1,0:T(8,128)} %bitcast.7, bf16[3,96,192]{2,1,0:T(8,128)(2,1)} %refs_2_.1, ...), custom_call_target="tpu_custom_call" | custom-call | tf_op jit(solution)/shard_map/layer/pallas_call | solution.py:835
  123.6 3.7 %finish.1 = (bf16[4,128,768]{2,1,0:T(8,128)(2,1)}, f32[4,128,768]{2,1,0:T(8,128)}, f32[3,96,192]{2,1,0:T(8,128)}, f32[2,192]{1,0:T(2,128)}, f32[192,96]{1,0:T(8,...) custom-call(bf16[4,128,768]{2,1,0:T(8,128)(2,1)} %get-tuple-element., ...), custom_call_target="tpu_custom_call" | custom-call | tf_op jit(solution)/shard_map/finish/pallas_call | solution.py:885

commit v6 on v5

--- a/solution.py
+++ b/solution.py
@@ -15,16 +15,16 @@
 F32 = jnp.float32
 BF16 = jnp.bfloat16
 BLOCKS = 4
-COPIES = 320
+COPIES = {(4, 2): 181}
 IN_RANGES = ((0, 768, False),)
 DOWN_RANGES = ((0, 384, True), (384, 768, False))
 IN_SUMS = ((0, 384, True), (384, 768, False))
 DOWN_SUMS = ((0, 384, True), (384, 768, False))
 QO_TURN = False
 QO_FIRST = False
-ORDER = (
-    "A0A1B0A2B1A3X5B2B3X2X6C0D0C1D1C2D2P0C3P1E0D3P2E1P3",
-    "E2F0E3G0F1H0F2G1G2H1I0F3H2G3X0I1H3X3I2I3X4X1",
+OA = "A0A1B0A2B1A3X5B2B3X2X6C0D0C1D1C2D2P0C3P1E0D3P2E1P3"
+OB = "E2F0E3G0F1H0F2G1G2H1I0F3H2X0G3I1H3X3I2I3X4X1"
+ORDER = (OA, OB,
 )
 
 
@@ -471,8 +471,7 @@
     wait_all(token_near)
     for e in range(1, ctxs):
         project_kv(e)
-    for gather in w_in:
-        gather.rest()
+    each(w_in, "rest")
 
     ott[0:cols] = jnp.zeros((cols, piece), F32)
     mt[0:cols] = jnp.zeros((cols, piece), F32)
@@ -565,8 +564,15 @@
         add_sum(4, grad * unit)
         add_sum(5, grad)
 
+    ready = set()
+
+    def cotangent_ready(b):
+        if b not in ready:
+            ready.add(b)
+            share_copy[1, b].wait_recv()
+
     def stage_g(b):
-        share_copy[1, b].wait_recv()
+        cotangent_ready(b)
         d_act = nn(dffn[b].reshape(rows_b, width), whole(wd, 0, width))
         dpre[b] = (d_act * slope[b]).astype(BF16)
         near_copy[2, b] = sum_start(2, b, nt(dpre[b], whole(wi, 0, width)))
@@ -588,6 +594,8 @@
     stages = dict(A=stage_a, B=stage_b, C=stage_c, D=stage_d, E=stage_e, P=stage_p, F=stage_f, G=stage_g, H=stage_h, I=stage_i)
 
     def down_grads():
+        for b in range(BLOCKS):
+            cotangent_ready(b)
         store_transposed(yt, dffn[...].reshape(piece, width))
         grad_product(2, 0, [(yt, act[...].reshape(piece, width))])
         each(g_down, "start", (0, 1))
@@ -857,36 +865,44 @@
      lo_out, tg_out, qkv_out, qv_out, out_out, in_out, down_out, v0, v1, v2, v3, v4, v5, v6, rms_out) = refs
     lo_out[...] = lo[...]
     tg_out[...] = tg[...].astype(F32)
-    qkv_out[0] = ga[:, 2 * cols:3 * cols]
-    qkv_out[1] = ga[:, 0:cols]
-    qkv_out[2] = ga[:, cols:2 * cols]
-    out_out[...] = jnp.transpose(ga[:, 3 * cols:])
-    in_out[...] = gi[...]
-    down_out[...] = gd[...]
-    qv_out[0:1] = small[18:19, 0:cols]
-    qv_out[1:2] = small[17:18, cols:2 * cols]
-    for row, ref in zip((0, 1, 2, 16, 3, 4, 5), (v0, v1, v2, v3, v4, v5, v6)):
-        ref[...] = small[row]
-    count = small[9:10, 0:1] * small.shape[1]
-    for i in range(3):
-        rms_out[0:1, i:i + 1] = jnp.sqrt(jnp.sum(small[6 + i:7 + i], axis=1, keepdims=True) / count)
+
+    @pl.when(pl.program_id(0) == 0)
+    def _():
+        qkv_out[0] = ga[:, 2 * cols:3 * cols]
+        qkv_out[1] = ga[:, 0:cols]
+        qkv_out[2] = ga[:, cols:2 * cols]
+        out_out[...] = jnp.transpose(ga[:, 3 * cols:])
+        in_out[...] = gi[...]
+        down_out[...] = gd[...]
+        qv_out[0:1] = small[18:19, 0:cols]
+        qv_out[1:2] = small[17:18, cols:2 * cols]
+        for row, ref in zip((0, 1, 2, 16, 3, 4, 5), (v0, v1, v2, v3, v4, v5, v6)):
+            ref[...] = small[row]
+        count = small[9:10, 0:1] * small.shape[1]
+        for i in range(3):
+            rms_out[0:1, i:i + 1] = jnp.sqrt(jnp.sum(small[6 + i:7 + i], axis=1, keepdims=True) / count)
 
 
 def run_finish(cols, *operands):
-    _, rows_b, width = operands[0].shape
+    blocks, rows_b, width = operands[0].shape
     chunk, hidden_cols = operands[3].shape
     shapes = [
-        ((BLOCKS, rows_b, width), BF16), ((BLOCKS, rows_b, width), F32), ((3, chunk, cols), F32), ((2, cols), F32),
+        ((blocks, rows_b, width), BF16), ((blocks, rows_b, width), F32), ((3, chunk, cols), F32), ((2, cols), F32),
         ((cols, chunk), F32), ((chunk, hidden_cols), F32), ((chunk, hidden_cols), F32),
         ((width,), F32), ((width,), F32), ((width,), F32), ((hidden_cols,), F32),
         ((width,), F32), ((width,), F32), ((width,), F32), ((1, 3), F32),
     ]
-    vmem = pl.BlockSpec(memory_space=pltpu.VMEM)
+    rows = pl.BlockSpec((1, rows_b, width), lambda i: (i, 0, 0))
+
+    def fixed(shape):
+        return pl.BlockSpec(shape, lambda i: (0,) * len(shape))
+
     return pl.pallas_call(
         functools.partial(finish_kernel, cols),
+        grid=(blocks,),
         out_shape=tuple(jax.ShapeDtypeStruct(*shape) for shape in shapes),
-        in_specs=[vmem] * len(operands),
-        out_specs=(vmem,) * len(shapes),
+        in_specs=[rows, rows] + [fixed(operand.shape) for operand in operands[2:]],
+        out_specs=(rows, rows) + tuple(fixed(shape[0]) for shape in shapes[2:]),
         name="finish",
     )(*operands)
 
@@ -916,7 +932,7 @@
     dims = (shards, ctxs, wctx, piece, width, chunk, heads)
     vectors = [out_bias, norm1_gain, norm1_shift, in_bias, down_bias, norm2_gain, norm2_shift]
     results = run_layer(
-        dims, COPIES, tokens.reshape(piece, width), out_cotangent.reshape(piece, width), *parts,
+        dims, COPIES.get((shards, ctxs), 320), tokens.reshape(piece, width), out_cotangent.reshape(piece, width), *parts,
         segment_ids, valid_mask, qv_bias, *vectors
     )
     if raw:

time: 128 us -> 126 us (0.984)
  Pallas kernels: 127 us -> 124 us
    pallas_call x1, Pallas kernels: 123 us -> 120 us  [run_layer(): pl.pallas_call(functools.partial(layer_kernel, dims), out_shape=(jax.Shap...]
where the time goes in v6:
time: 126 us; the launch traced here: 125 us
  Pallas kernels  124 us (98%)
    pallas_call x1, Pallas kernels, run_layer(): pl.pallas_call(functools.partial(layer_kernel, dims), out_shape=(jax.Shap...  120 us
    pallas_call x1, Pallas kernels, run_finish(): pl.pallas_call(functools.partial(finish_kernel, cols), grid=(blocks,), ou...  4.79 us

profile of v6, /device:TPU:0, one launch (start us, length us, event | category | flops | bytes accessed | tf_op | source)
XLA Modules:
  0.0 125.3 jit_solution(6982969968593947034)
XLA Ops:
  0.7 119.7 %layer.1 = (bf16[4,128,768]{2,1,0:T(8,128)(2,1)}, bf16[4,128,768]{2,1,0:T(8,128)(2,1)}, f32[96,768]{1,0:T(8,128)}, f32[96,768]{1,0:T(8,128)}, f32[96,768]{1,0:T(8,128)}, /*index=5*/f32[24,768]{1,0:T(8,128)}) custom-call(bf16[512,768]{1,0:T(8,128)(2,1)} %bitcast.8, f32[512,768]{1,0:T(8,128)} %bitcast.7, bf16[3,96,192]{2,1,0:T(8,128)(2,1)} %refs_2_.1, ...), custom_call_target="tpu_custom_call" | custom-call | tf_op jit(solution)/shard_map/layer/pallas_call | solution.py:843
  120.4 4.8 %finish.1 = (bf16[4,128,768]{2,1,0:T(8,128)(2,1)}, f32[4,128,768]{2,1,0:T(8,128)}, f32[3,96,192]{2,1,0:T(8,128)}, f32[2,192]{1,0:T(2,128)}, f32[192,96]{1,0:T(8,...) custom-call(bf16[4,128,768]{2,1,0:T(8,128)(2,1)} %get-tuple-element., ...), custom_call_target="tpu_custom_call" | custom-call | tf_op jit(solution)/shard_map/finish/pallas_call | solution.py:900

commit v7 on v6

--- a/solution.py
+++ b/solution.py
@@ -15,6 +15,7 @@
 F32 = jnp.float32
 BF16 = jnp.bfloat16
 BLOCKS = 4
+POOL = 96
 COPIES = {(4, 2): 181}
 IN_RANGES = ((0, 768, False),)
 DOWN_RANGES = ((0, 384, True), (384, 768, False))
@@ -71,10 +72,12 @@
 
     def send(self, source, target, where, when=None, place=None):
         number = len(self.copies)
+        if number >= POOL:
+            self.sent(number - POOL)
         copy = pltpu.make_async_remote_copy(
             src_ref=source,
             dst_ref=target,
-            send_sem=self.send_sems.at[number],
+            send_sem=self.send_sems.at[number % POOL],
             recv_sem=self.recv_sems.at[number if place is None else place],
             device_id=where,
             device_id_type=pl.DeviceIdType.MESH,
@@ -88,11 +91,15 @@
         return copy
 
     def finish(self):
-        for copy, when in self.copies:
-            if when is None:
-                copy.wait_send()
-            else:
-                pl.when(when)(copy.wait_send)
+        for number in range(max(0, len(self.copies) - POOL), len(self.copies)):
+            self.sent(number)
+
+    def sent(self, number):
+        copy, when = self.copies[number]
+        if when is None:
+            copy.wait_send()
+        else:
+            pl.when(when)(copy.wait_send)
 
 
 def layer_kernel(dims, *refs):
@@ -837,7 +844,7 @@
         V((ctxs, 8, width), F32), V((shards, 8, width), F32),
         V((3, chunk, cols), BF16), V((cols, chunk), BF16), V((8, piece), F32), V((8, 2 * cols), F32),
         V((8, piece), F32), V((ctxs - 1, 8, piece), F32), V((8, piece), F32), V((ctxs - 1, 8, piece), F32),
-        pltpu.SemaphoreType.DMA((BLOCKS + 5,)), pltpu.SemaphoreType.DMA((copies,)),
+        pltpu.SemaphoreType.DMA((BLOCKS + 5,)), pltpu.SemaphoreType.DMA((min(copies, POOL),)),
         pltpu.SemaphoreType.DMA((copies,)),
     ]
     return pl.pallas_call(

time: 126 us -> 125 us (level)
  no operation moved by 1% of the time
where the time goes in v7:
time: 125 us
  Pallas kernels  124 us (99%)
    pallas_call x1, Pallas kernels, run_layer(): pl.pallas_call(functools.partial(layer_kernel, dims), out_shape=(jax.Shap...  119 us
    pallas_call x1, Pallas kernels, run_finish(): pl.pallas_call(functools.partial(finish_kernel, cols), grid=(blocks,), ou...  4.79 us

profile of v7, /device:TPU:0, one launch (start us, length us, event | category | flops | bytes accessed | tf_op | source)
XLA Modules:
  0.0 124.5 jit_solution(12791158112893769608)
XLA Ops:
  0.7 118.9 %layer.1 = (bf16[4,128,768]{2,1,0:T(8,128)(2,1)}, bf16[4,128,768]{2,1,0:T(8,128)(2,1)}, f32[96,768]{1,0:T(8,128)}, f32[96,768]{1,0:T(8,128)}, f32[96,768]{1,0:T(8,128)}, /*index=5*/f32[24,768]{1,0:T(8,128)}) custom-call(bf16[512,768]{1,0:T(8,128)(2,1)} %bitcast.8, f32[512,768]{1,0:T(8,128)} %bitcast.7, bf16[3,96,192]{2,1,0:T(8,128)(2,1)} %refs_2_.1, ...), custom_call_target="tpu_custom_call" | custom-call | tf_op jit(solution)/shard_map/layer/pallas_call | solution.py:850
  119.6 4.8 %finish.1 = (bf16[4,128,768]{2,1,0:T(8,128)(2,1)}, f32[4,128,768]{2,1,0:T(8,128)}, f32[3,96,192]{2,1,0:T(8,128)}, f32[2,192]{1,0:T(2,128)}, f32[192,96]{1,0:T(8,...) custom-call(bf16[4,128,768]{2,1,0:T(8,128)(2,1)} %get-tuple-element., ...), custom_call_target="tpu_custom_call" | custom-call | tf_op jit(solution)/shard_map/finish/pallas_call | solution.py:907
